TPU v7x, 512 devices: a whole 4x8x8 slice. The times are simulated.
512 devices in a mesh: sub: 128 (over y, z, core), grp: 4 (over x).
Axes of the slice: x: 4, y: 8, z: 8, core: 2. Of those that a mesh axis runs over, the one named last changes fastest.
Arguments:
- deflation: bfloat16 [512, 512, 4, 128], P(None, 'sub', 'grp'), may hold values from -0.045643546 to 0.045643546
- shift_field: float32 [512, 4, 128], P('sub', 'grp'), may hold values from 0.5 to 8
- counts: int32 [128], P('sub'), may hold values from 128 to 512, as said below
- right_sides: float32 [65536, 256], P(('sub', 'grp')), may hold values from -6 to 6
Outputs:
- coarse_solution: float32 [65536, 256], P(('sub', 'grp'))
Inputs may be any that keep to these rules, and one draw needn't show every extreme that they name: `counts`: live deflation vectors of each subdomain; some subdomain has 512 and some 512 // 4.
All inputs are finite; a program needn't handle non-finite values.
Results may differ from a plain program's by a relative error of at most 0.0014.
Values may be sent and summed in bfloat16 or wider, within the bound.
No kernel may reach another device: no remote copies, remote signals or barrier semaphores. Data moves between devices by JAX's collectives and lax.ppermute only.
A program may use at most 64 MiB of HBM per device.

v0:
```python
import jax
import jax.numpy as jnp
from jax import lax
from jax.sharding import PartitionSpec as P

SWEEPS = 6


damping = 0.7


def extended(cells, sides, width):
    for axis, dim in sides:
        count = lax.axis_size(axis)
        ends = count - 1
        head = lax.slice_in_dim(cells, 0, width, axis=dim)
        tail = lax.slice_in_dim(cells, cells.shape[dim] - width, cells.shape[dim], axis=dim)
        cells = jnp.concatenate(
            [
                lax.ppermute(tail, axis, [(i, (i + 1) % count) for i in range(ends)]),
                cells,
                lax.ppermute(head, axis, [((i + 1) % count, i) for i in range(ends)]),
            ],
            axis=dim,
        )
    return cells


def smooth_last(values):
    width_x = values.shape[-1]
    positions = lax.iota(jnp.int32, width_x)
    left_side = jnp.where(positions >= 1, jnp.roll(values, 1, axis=-1), 0.0)
    right_side = jnp.where(positions < width_x - 1, jnp.roll(values, -1, axis=-1), 0.0)
    return values + 0.5 * (left_side + right_side)


def smooth_valid(values, which_axis):
    length = values.shape[which_axis]
    center = lax.slice_in_dim(values, 1, length - 1, axis=which_axis)
    lower = lax.slice_in_dim(values, 0, length - 2, axis=which_axis)
    upper = lax.slice_in_dim(values, 2, length, axis=which_axis)
    return center + 0.5 * (lower + upper)


def contract(left_part, right_part):
    return lax.dot_general(
        left_part, right_part, (((1,), (1,)), ((), ())), preferred_element_type=jnp.float32
    )


def on_device(deflation, shift_field, counts, right_sides):
    slot_count = deflation.shape[0]
    planes = deflation.shape[1]
    block_rows = right_sides.shape[0]
    live_count = counts[0]
    slot_ids = lax.iota(jnp.int32, slot_count)
    live_slots = slot_ids < live_count
    masked = jnp.where(live_slots[:, None, None, None], deflation, jnp.zeros((), deflation.dtype))
    padded = extended(masked, (("sub", 1), ("grp", 2)), 1)
    along_x = smooth_last(padded.astype(jnp.float32))
    along_y = smooth_valid(along_x, 2)
    inner_part = along_y[:, 1 : planes + 1]
    with_rims = jnp.pad(inner_part, ((0, 0), (1, 1), (0, 0), (0, 0)))
    along_z = smooth_valid(with_rims, 1)
    own_field = masked.astype(jnp.float32)
    images = ((16.0 + shift_field) * own_field - 2.0 * along_z).astype(jnp.bfloat16)
    above_plane = along_y[:, planes + 1].astype(jnp.bfloat16).reshape(slot_count, -1)
    below_plane = along_y[:, 0].astype(jnp.bfloat16).reshape(slot_count, -1)
    flat_vectors = masked.reshape(slot_count, -1)
    flat_images = images.reshape(slot_count, -1)
    top_plane = masked[:, planes - 1].reshape(slot_count, -1)
    bottom = masked[:, 0].reshape(slot_count, -1)
    row_start = lax.axis_index("grp") * block_rows
    lower_part = -contract(bottom, below_plane)
    middle = contract(flat_vectors, flat_images)
    upper_part = -contract(top_plane, above_plane)
    summed = lax.psum(jnp.concatenate([lower_part, middle, upper_part], axis=1), "grp")
    own_rows = lax.dynamic_slice_in_dim(summed, row_start, block_rows, 0)
    row_slot = row_start + lax.iota(jnp.int32, block_rows)
    row_padded = row_slot >= live_count
    columns = lax.iota(jnp.int32, 3 * slot_count)
    pad_mask = (columns[None, :] == row_slot[:, None] + slot_count) & row_padded[:, None]
    matrix = own_rows + jnp.where(pad_mask, 1.0, 0.0).astype(jnp.float32)
    block = lax.dynamic_slice_in_dim(matrix, slot_count + row_start, block_rows, 1)
    factor = jnp.linalg.cholesky(block)
    rhs_masked = jnp.where(row_padded[:, None], 0.0, right_sides)
    current = damping * jax.scipy.linalg.cho_solve((factor, True), rhs_masked)
    for sweep in range(SWEEPS - 1):
        slab_iter = lax.all_gather(current, "grp", axis=0, tiled=True)
        stacked = extended(slab_iter, (("sub", 0),), slot_count)
        product = jnp.dot(matrix, stacked, precision=lax.Precision.HIGHEST)
        update = jax.scipy.linalg.cho_solve((factor, True), rhs_masked - product)
        current = current + damping * update
    return current


def solution(mesh):
    in_specs = (
        P(None, "sub", "grp", None),
        P("sub", "grp", None),
        P("sub"),
        P(("sub", "grp"), None),
    )
    out_specs = P(("sub", "grp"), None)
    return jax.shard_map(
        on_device, mesh=mesh, in_specs=in_specs, out_specs=out_specs, check_vma=False
    )
```

profile of v0, /device:TPU:32, one launch (start us, length us, event | category | flops | bytes accessed | tf_op | source)
XLA Modules:
  0.0 334.7 jit_solution(12672076936665335172)
XLA Ops:
  7.2 1.2 copy_select_fusion
  8.4 1.9 collective-permute-start
  10.4 10.3 %collective-permute-start.1 = (bf16[512,1,1,128]{3,0,2,1:T(8,128)(2,1)S(1)}, bf16[512,1,1,128]{3,0,2,1:T(8,128)(2,1)S(1)}, u32[]{:S(2)}, u32[]{:S(2)}) collective-permute-start(bf16[512,1,1,128]{3,0,2,1:T(8,128)(2,1)S(1)} %get-tuple-element.13), channel_id=1, source_target_pairs={{4,0},{8,4},{12,8},{16,12},{20,16},{24,20},{28,24},{32,28},{36,32}... | collective-permute-start | bytes 393224 | tf_op jit(solution)/shard_map/ppermute | solution.py:22
  20.6 0.7 collective-permute-done
  21.4 1.8 collective-permute-done.1
  23.2 4.3 %collective-permute-start.2 = (bf16[512,6,1,128]{3,0,2,1:T(8,128)(2,1)S(1)}, bf16[512,6,1,128]{3,0,2,1:T(8,128)(2,1)}, u32[]{:S(2)}, u32[]{:S(2)}) collective-permute-start(bf16[512,6,1,128]{3,0,2,1:T(8,128)(2,1)S(1)} %pad_maximum_fusion.1), channel_id=1, source_target_pairs={{0,1},{1,2},{2,3},{4,5},{5,6},{6,7},{8,9},{9,10},{10,11},{12,13},{... | collective-permute-start | bytes 2359304 | tf_op jit(solution)/shard_map/ppermute | solution.py:20
  27.5 1.3 collective-permute-start.3
  28.9 10.7 %collective-permute-done.2 = bf16[512,6,1,128]{3,0,2,1:T(8,128)(2,1)} collective-permute-done((bf16[512,6,1,128]{3,0,2,1:T(8,128)(2,1)S(1)}, bf16[512,6,1,128]{3,0,2,1:T(8,128)(2,1)}, u32[]{:S(2)}, u32[]{:S(2)}) %collective-permute-start.2) | collective-permute-done | bytes 786464 | tf_op jit(solution)/shard_map/ppermute | solution.py:20
  39.6 5.1 %collective-permute-done.3 = bf16[512,6,1,128]{3,0,2,1:T(8,128)(2,1)} collective-permute-done((bf16[512,6,1,128]{3,0,2,1:T(8,128)(2,1)S(1)}, bf16[512,6,1,128]{3,0,2,1:T(8,128)(2,1)}, u32[]{:S(2)}, u32[]{:S(2)}) %collective-permute-start.3) | collective-permute-done | bytes 786464 | tf_op jit(solution)/shard_map/ppermute | solution.py:22
  44.7 1.6 maximum_convert_fusion
  46.3 1.7 fusion.108
  48.0 3.8 %fusion.107 = (f32[512,6,3,127]{3,0,2,1:T(8,128)S(1)}, f32[512,6,3,127]{3,0,2,1:T(8,128)}) fusion(f32[512,6,3,128]{3,0,2,1:T(8,128)S(1)} %maximum_convert_fusion), kind=kLoop, calls=%fused_computation.129 | loop fusion | bytes 18726912 | tf_op jit(solution)/shard_map/jit(_roll_static)/slice | solution.py:33
  51.8 5.0 %fusion.2 = f32[512,6,3,128]{3,0,2,1:T(8,128)S(1)} fusion(f32[512,6,3,127]{3,0,2,1:T(8,128)} %get-tuple-element.9, f32[512,6,3,1]{3,0,2,1:T(8,128)S(1)} %get-tuple-element.11, f32[512,6,3,1]{3,0,2,1:T(8,128)S(1)} %get-tuple-element.10, f32[512,6,3,127]{3,0,2,1:T(8,128)S(1)} %get-tuple-element.8, pred[128]{0:T(512)(128)(4,1)S(1)} %get-tuple-element.14, ...), kind=kLoop, calls=%fused_computation.3 | loop fusion | flops 14155776 | bytes 16515328 | tf_op jit(solution)/shard_map/add | solution.py:34
  57.0 0.3 convolution_negate_fusion.1
  57.3 0.3 convolution_negate_fusion
  57.7 0.5 convolution_bitcast_fusion
  58.2 2.0 pad_maximum_fusion
  60.3 88.7 %all-reduce.3.cloned.1.call-done = f32[512,1536]{0,1:T(8,128)} async-done(((f32[512,1536]{0,1:T(8,128)}), f32[512,1536]{0,1:T(8,128)}) %all-reduce.3.cloned.1.call-update) | async-done | bytes 3145744 | tf_op jit(solution)/shard_map/psum | solution.py:77
  149.0 1.3 select_add_fusion
  150.4 11.7 %cholesky.18 = f32[128,128]{1,0:T(8,128)S(1)} custom-call(f32[128,128]{1,0:T(8,128)S(1)} %fusion.89), custom_call_target="Cholesky" | custom-call | tf_op jit(solution)/shard_map/jit(cholesky)/cholesky | solution.py:85
  162.2 0.6 compare_reduce_fusion
  162.8 0.7 fusion.71
  163.5 9.8 %custom-call.13 = f32[1,128,128]{1,2,0:T(8,128)S(1)} custom-call(f32[1,128,128]{2,1,0:T(8,128)S(1)} %fusion.71), custom_call_target="InvertDiagBlocksLowerTriangular" | custom-call | tf_op jit(solution)/shard_map/jit(_cho_solve)/triangular_solve | solution.py:87
  173.3 0.3 fusion.69
  173.9 13.5 %all_gather.15 = f32[512,256]{1,0:T(8,128)S(1)} all-gather(f32[128,256]{1,0:T(8,128)S(1)} %convolution_multiply_fusion.5), channel_id=1, replica_groups=mesh['sub'=128,'grp'=4] {'grp'}, dimensions={0}, use_global_device_ids=true | all-gather | bytes 655360 | tf_op jit(solution)/shard_map/all_gather | solution.py:89
  187.4 1.9 collective-permute-start.4
  189.3 7.0 %collective-permute-start.5 = (f32[512,256]{1,0:T(8,128)S(1)}, f32[512,256]{1,0:T(8,128)S(1)}, u32[]{:S(2)}, u32[]{:S(2)}) collective-permute-start(f32[512,256]{1,0:T(8,128)S(1)} %all_gather.15), channel_id=1, source_target_pairs={{4,0},{8,4},{12,8},{16,12},{20,16},{24,20},{28,24},{32,28},{36,32}... | collective-permute-start | bytes 1572872 | tf_op jit(solution)/shard_map/ppermute | solution.py:22
  196.3 4.9 %collective-permute-done.4 = f32[512,256]{1,0:T(8,128)S(1)} collective-permute-done((f32[512,256]{1,0:T(8,128)S(1)}, f32[512,256]{1,0:T(8,128)S(1)}, u32[]{:S(2)}, u32[]{:S(2)}) %collective-permute-start.4) | collective-permute-done | bytes 524320 | tf_op jit(solution)/shard_map/ppermute | solution.py:20
  201.2 1.8 collective-permute-done.5
  203.0 1.5 fusion.47
  204.4 0.3 fusion.85
  204.8 0.3 fusion.50
  205.0 12.8 %all_gather.16 = f32[512,256]{1,0:T(8,128)S(1)} all-gather(f32[128,256]{1,0:T(8,128)S(1)} %fusion.50), channel_id=1, replica_groups=mesh['sub'=128,'grp'=4] {'grp'}, dimensions={0}, use_global_device_ids=true | all-gather | bytes 655360 | tf_op jit(solution)/shard_map/all_gather | solution.py:89
  217.8 1.9 collective-permute-start.6
  219.7 7.2 %collective-permute-start.7 = (f32[512,256]{1,0:T(8,128)S(1)}, f32[512,256]{1,0:T(8,128)S(1)}, u32[]{:S(2)}, u32[]{:S(2)}) collective-permute-start(f32[512,256]{1,0:T(8,128)S(1)} %all_gather.16), channel_id=1, source_target_pairs={{4,0},{8,4},{12,8},{16,12},{20,16},{24,20},{28,24},{32,28},{36,32}... | collective-permute-start | bytes 1572872 | tf_op jit(solution)/shard_map/ppermute | solution.py:22
  226.9 4.7 %collective-permute-done.6 = f32[512,256]{1,0:T(8,128)S(1)} collective-permute-done((f32[512,256]{1,0:T(8,128)S(1)}, f32[512,256]{1,0:T(8,128)S(1)}, u32[]{:S(2)}, u32[]{:S(2)}) %collective-permute-start.6) | collective-permute-done | bytes 524320 | tf_op jit(solution)/shard_map/ppermute | solution.py:20
  231.6 1.8 collective-permute-done.7
  233.4 1.5 fusion.44
  234.8 0.3 fusion.82
  235.2 0.3 fusion.51
  235.4 13.3 %all_gather.17 = f32[512,256]{1,0:T(8,128)S(1)} all-gather(f32[128,256]{1,0:T(8,128)S(1)} %fusion.51), channel_id=1, replica_groups=mesh['sub'=128,'grp'=4] {'grp'}, dimensions={0}, use_global_device_ids=true | all-gather | bytes 655360 | tf_op jit(solution)/shard_map/all_gather | solution.py:89
  248.8 1.9 collective-permute-start.8
  250.7 7.0 %collective-permute-start.9 = (f32[512,256]{1,0:T(8,128)S(1)}, f32[512,256]{1,0:T(8,128)S(1)}, u32[]{:S(2)}, u32[]{:S(2)}) collective-permute-start(f32[512,256]{1,0:T(8,128)S(1)} %all_gather.17), channel_id=1, source_target_pairs={{4,0},{8,4},{12,8},{16,12},{20,16},{24,20},{28,24},{32,28},{36,32}... | collective-permute-start | bytes 1572872 | tf_op jit(solution)/shard_map/ppermute | solution.py:22
  257.6 4.9 %collective-permute-done.8 = f32[512,256]{1,0:T(8,128)S(1)} collective-permute-done((f32[512,256]{1,0:T(8,128)S(1)}, f32[512,256]{1,0:T(8,128)S(1)}, u32[]{:S(2)}, u32[]{:S(2)}) %collective-permute-start.8) | collective-permute-done | bytes 524320 | tf_op jit(solution)/shard_map/ppermute | solution.py:20
  262.6 1.8 collective-permute-done.9
  264.3 1.5 fusion.41
  265.8 0.3 fusion.79
  266.1 0.3 fusion.52
  266.4 12.8 %all_gather.18 = f32[512,256]{1,0:T(8,128)S(1)} all-gather(f32[128,256]{1,0:T(8,128)S(1)} %fusion.52), channel_id=1, replica_groups=mesh['sub'=128,'grp'=4] {'grp'}, dimensions={0}, use_global_device_ids=true | all-gather | bytes 655360 | tf_op jit(solution)/shard_map/all_gather | solution.py:89
  279.2 1.9 collective-permute-start.10
  281.1 7.0 %collective-permute-start.11 = (f32[512,256]{1,0:T(8,128)S(1)}, f32[512,256]{1,0:T(8,128)S(1)}, u32[]{:S(2)}, u32[]{:S(2)}) collective-permute-start(f32[512,256]{1,0:T(8,128)S(1)} %all_gather.18), channel_id=1, source_target_pairs={{4,0},{8,4},{12,8},{16,12},{20,16},{24,20},{28,24},{32,28},{36,32}... | collective-permute-start | bytes 1572872 | tf_op jit(solution)/shard_map/ppermute | solution.py:22
  288.0 4.9 %collective-permute-done.10 = f32[512,256]{1,0:T(8,128)S(1)} collective-permute-done((f32[512,256]{1,0:T(8,128)S(1)}, f32[512,256]{1,0:T(8,128)S(1)}, u32[]{:S(2)}, u32[]{:S(2)}) %collective-permute-start.10) | collective-permute-done | bytes 524320 | tf_op jit(solution)/shard_map/ppermute | solution.py:20
  293.0 1.8 collective-permute-done.11
  294.7 1.5 fusion.38
  296.2 0.3 fusion.76
  296.5 0.3 fusion.53
  296.8 12.8 %all_gather.19 = f32[512,256]{1,0:T(8,128)S(1)} all-gather(f32[128,256]{1,0:T(8,128)S(1)} %fusion.53), channel_id=1, replica_groups=mesh['sub'=128,'grp'=4] {'grp'}, dimensions={0}, use_global_device_ids=true | all-gather | bytes 655360 | tf_op jit(solution)/shard_map/all_gather | solution.py:89
  309.6 1.9 collective-permute-start.12
  311.5 7.0 %collective-permute-start.13 = (f32[512,256]{1,0:T(8,128)S(1)}, f32[512,256]{1,0:T(8,128)S(1)}, u32[]{:S(2)}, u32[]{:S(2)}) collective-permute-start(f32[512,256]{1,0:T(8,128)S(1)} %all_gather.19), channel_id=1, source_target_pairs={{4,0},{8,4},{12,8},{16,12},{20,16},{24,20},{28,24},{32,28},{36,32}... | collective-permute-start | bytes 1572872 | tf_op jit(solution)/shard_map/ppermute | solution.py:22
  318.5 4.9 %collective-permute-done.12 = f32[512,256]{1,0:T(8,128)S(1)} collective-permute-done((f32[512,256]{1,0:T(8,128)S(1)}, f32[512,256]{1,0:T(8,128)S(1)}, u32[]{:S(2)}, u32[]{:S(2)}) %collective-permute-start.12) | collective-permute-done | bytes 524320 | tf_op jit(solution)/shard_map/ppermute | solution.py:20
  323.4 1.8 collective-permute-done.13
  325.1 1.5 fusion.35
  326.6 0.3 fusion.73
  326.9 0.9 fusion.54
  (24 shorter events, 0.9 us)
Async XLA Ops:
  6.5 22.3 %copy-start.3 = (f32[4,1,128]{2,1,0:T(1,128)S(1)}, f32[4,1,128]{2,1,0:T(1,128)}, u32[]{:S(2)}) copy-start(f32[4,1,128]{2,1,0:T(1,128)} %param.7) | copy-start | bytes 6148
  6.5 142.4 %all-reduce.3.cloned.1.call-start = ((), (), s32[]{:S(2)}) async-start(), calls=%async_computation | async-start | bytes 6291456 | tf_op jit(solution)/shard_map/psum | solution.py:77
  8.4 12.9 %collective-permute-start = (bf16[512,1,1,128]{3,0,2,1:T(8,128)(2,1)S(1)}, bf16[512,1,1,128]{3,0,2,1:T(8,128)(2,1)S(1)}, u32[]{:S(2)}, u32[]{:S(2)}) collective-permute-start(bf16[512,1,1,128]{3,0,2,1:T(8,128)(2,1)S(1)} %get-tuple-element.12), channel_id=1, source_target_pairs={{0,4},{4,8},{8,12},{12,16},{16,20},{20,24},{24,28},{28,32},{32,36}... | collective-permute-start | bytes 393224 | tf_op jit(solution)/shard_map/ppermute | solution.py:20
  10.4 12.8 %collective-permute-start.1 = (bf16[512,1,1,128]{3,0,2,1:T(8,128)(2,1)S(1)}, bf16[512,1,1,128]{3,0,2,1:T(8,128)(2,1)S(1)}, u32[]{:S(2)}, u32[]{:S(2)}) collective-permute-start(bf16[512,1,1,128]{3,0,2,1:T(8,128)(2,1)S(1)} %get-tuple-element.13), channel_id=1, source_target_pairs={{4,0},{8,4},{12,8},{16,12},{20,16},{24,20},{28,24},{32,28},{36,32}... | collective-permute-start | bytes 393224 | tf_op jit(solution)/shard_map/ppermute | solution.py:22
  21.3 23.3 %copy-start.1 = (bf16[512,1,1,128]{3,0,2,1:T(8,128)(2,1)}, bf16[512,1,1,128]{3,0,2,1:T(8,128)(2,1)S(1)}, u32[]{:S(2)}) copy-start(bf16[512,1,1,128]{3,0,2,1:T(8,128)(2,1)S(1)} %collective-permute-done) | copy-start | bytes 393220
  23.1 21.5 %copy-start.2 = (bf16[512,1,1,128]{3,0,2,1:T(8,128)(2,1)}, bf16[512,1,1,128]{3,0,2,1:T(8,128)(2,1)S(1)}, u32[]{:S(2)}) copy-start(bf16[512,1,1,128]{3,0,2,1:T(8,128)(2,1)S(1)} %collective-permute-done.1) | copy-start | bytes 393220
  23.2 16.3 %collective-permute-start.2 = (bf16[512,6,1,128]{3,0,2,1:T(8,128)(2,1)S(1)}, bf16[512,6,1,128]{3,0,2,1:T(8,128)(2,1)}, u32[]{:S(2)}, u32[]{:S(2)}) collective-permute-start(bf16[512,6,1,128]{3,0,2,1:T(8,128)(2,1)S(1)} %pad_maximum_fusion.1), channel_id=1, source_target_pairs={{0,1},{1,2},{2,3},{4,5},{5,6},{6,7},{8,9},{9,10},{10,11},{12,13},{... | collective-permute-start | bytes 2359304 | tf_op jit(solution)/shard_map/ppermute | solution.py:20
  27.5 17.1 %collective-permute-start.3 = (bf16[512,6,1,128]{3,0,2,1:T(8,128)(2,1)S(1)}, bf16[512,6,1,128]{3,0,2,1:T(8,128)(2,1)}, u32[]{:S(2)}, u32[]{:S(2)}) collective-permute-start(bf16[512,6,1,128]{3,0,2,1:T(8,128)(2,1)S(1)} %pad_maximum_fusion.1), channel_id=1, source_target_pairs={{1,0},{2,1},{3,2},{5,4},{6,5},{7,6},{9,8},{10,9},{11,10},{13,12},{... | collective-permute-start | bytes 2359304 | tf_op jit(solution)/shard_map/ppermute | solution.py:22
  60.2 113.1 %copy-start = (f32[128,256]{1,0:T(8,128)S(1)}, f32[128,256]{1,0:T(8,128)}, u32[]{:S(2)}) copy-start(f32[128,256]{1,0:T(8,128)} %param.9) | copy-start | bytes 393220
  187.4 13.8 %collective-permute-start.4 = (f32[512,256]{1,0:T(8,128)S(1)}, f32[512,256]{1,0:T(8,128)S(1)}, u32[]{:S(2)}, u32[]{:S(2)}) collective-permute-start(f32[512,256]{1,0:T(8,128)S(1)} %all_gather.15), channel_id=1, source_target_pairs={{0,4},{4,8},{8,12},{12,16},{16,20},{20,24},{24,28},{28,32},{32,36}... | collective-permute-start | bytes 1572872 | tf_op jit(solution)/shard_map/ppermute | solution.py:20
  189.3 13.6 %collective-permute-start.5 = (f32[512,256]{1,0:T(8,128)S(1)}, f32[512,256]{1,0:T(8,128)S(1)}, u32[]{:S(2)}, u32[]{:S(2)}) collective-permute-start(f32[512,256]{1,0:T(8,128)S(1)} %all_gather.15), channel_id=1, source_target_pairs={{4,0},{8,4},{12,8},{16,12},{20,16},{24,20},{28,24},{32,28},{36,32}... | collective-permute-start | bytes 1572872 | tf_op jit(solution)/shard_map/ppermute | solution.py:22
  217.8 13.8 %collective-permute-start.6 = (f32[512,256]{1,0:T(8,128)S(1)}, f32[512,256]{1,0:T(8,128)S(1)}, u32[]{:S(2)}, u32[]{:S(2)}) collective-permute-start(f32[512,256]{1,0:T(8,128)S(1)} %all_gather.16), channel_id=1, source_target_pairs={{0,4},{4,8},{8,12},{12,16},{16,20},{20,24},{24,28},{28,32},{32,36}... | collective-permute-start | bytes 1572872 | tf_op jit(solution)/shard_map/ppermute | solution.py:20
  219.7 13.6 %collective-permute-start.7 = (f32[512,256]{1,0:T(8,128)S(1)}, f32[512,256]{1,0:T(8,128)S(1)}, u32[]{:S(2)}, u32[]{:S(2)}) collective-permute-start(f32[512,256]{1,0:T(8,128)S(1)} %all_gather.16), channel_id=1, source_target_pairs={{4,0},{8,4},{12,8},{16,12},{20,16},{24,20},{28,24},{32,28},{36,32}... | collective-permute-start | bytes 1572872 | tf_op jit(solution)/shard_map/ppermute | solution.py:22
  248.8 13.8 %collective-permute-start.8 = (f32[512,256]{1,0:T(8,128)S(1)}, f32[512,256]{1,0:T(8,128)S(1)}, u32[]{:S(2)}, u32[]{:S(2)}) collective-permute-start(f32[512,256]{1,0:T(8,128)S(1)} %all_gather.17), channel_id=1, source_target_pairs={{0,4},{4,8},{8,12},{12,16},{16,20},{20,24},{24,28},{28,32},{32,36}... | collective-permute-start | bytes 1572872 | tf_op jit(solution)/shard_map/ppermute | solution.py:20
  250.7 13.6 %collective-permute-start.9 = (f32[512,256]{1,0:T(8,128)S(1)}, f32[512,256]{1,0:T(8,128)S(1)}, u32[]{:S(2)}, u32[]{:S(2)}) collective-permute-start(f32[512,256]{1,0:T(8,128)S(1)} %all_gather.17), channel_id=1, source_target_pairs={{4,0},{8,4},{12,8},{16,12},{20,16},{24,20},{28,24},{32,28},{36,32}... | collective-permute-start | bytes 1572872 | tf_op jit(solution)/shard_map/ppermute | solution.py:22
  279.2 13.8 %collective-permute-start.10 = (f32[512,256]{1,0:T(8,128)S(1)}, f32[512,256]{1,0:T(8,128)S(1)}, u32[]{:S(2)}, u32[]{:S(2)}) collective-permute-start(f32[512,256]{1,0:T(8,128)S(1)} %all_gather.18), channel_id=1, source_target_pairs={{0,4},{4,8},{8,12},{12,16},{16,20},{20,24},{24,28},{28,32},{32,36}... | collective-permute-start | bytes 1572872 | tf_op jit(solution)/shard_map/ppermute | solution.py:20
  281.1 13.6 %collective-permute-start.11 = (f32[512,256]{1,0:T(8,128)S(1)}, f32[512,256]{1,0:T(8,128)S(1)}, u32[]{:S(2)}, u32[]{:S(2)}) collective-permute-start(f32[512,256]{1,0:T(8,128)S(1)} %all_gather.18), channel_id=1, source_target_pairs={{4,0},{8,4},{12,8},{16,12},{20,16},{24,20},{28,24},{32,28},{36,32}... | collective-permute-start | bytes 1572872 | tf_op jit(solution)/shard_map/ppermute | solution.py:22
  309.6 13.8 %collective-permute-start.12 = (f32[512,256]{1,0:T(8,128)S(1)}, f32[512,256]{1,0:T(8,128)S(1)}, u32[]{:S(2)}, u32[]{:S(2)}) collective-permute-start(f32[512,256]{1,0:T(8,128)S(1)} %all_gather.19), channel_id=1, source_target_pairs={{0,4},{4,8},{8,12},{12,16},{16,20},{20,24},{24,28},{28,32},{32,36}... | collective-permute-start | bytes 1572872 | tf_op jit(solution)/shard_map/ppermute | solution.py:20
  311.5 13.6 %collective-permute-start.13 = (f32[512,256]{1,0:T(8,128)S(1)}, f32[512,256]{1,0:T(8,128)S(1)}, u32[]{:S(2)}, u32[]{:S(2)}) collective-permute-start(f32[512,256]{1,0:T(8,128)S(1)} %all_gather.19), channel_id=1, source_target_pairs={{4,0},{8,4},{12,8},{16,12},{20,16},{24,20},{28,24},{32,28},{36,32}... | collective-permute-start | bytes 1572872 | tf_op jit(solution)/shard_map/ppermute | solution.py:22
Sparse Core Ops, SparseCore 0:
  60.3 88.5 all-reduce.2
where the time goes:
time: 335 us
  waiting for transfers between devices  140 us (42%)
  blocking collectives  65.2 us (19%)
  starting transfers between devices  62.4 us (19%)
  other arithmetic  34.3 us (10%)
  between operations  14.5 us (4%)
  matrix products  12.5 us (4%)
  local copies, waits for them, and re-layouts  5.69 us (2%)
    psum x1, waiting for transfers between devices, on_device(): lax.psum(jnp.concatenate([lower_part, middle, upper_part], axis=1), 'grp')  88.7 us
    all_gather x5, blocking collectives, on_device(): slab_iter = lax.all_gather(current, 'grp', axis=0, tiled=True)  65.2 us
    ppermute x7, starting transfers between devices, extended(): lax.ppermute(head, axis, [((i + 1) % count, i) for i in range(ends)])  46.6 us
    ppermute x7, waiting for transfers between devices, extended(): lax.ppermute(tail, axis, [(i, (i + 1) % count) for i in range(ends)])  35.8 us
    ppermute x7, starting transfers between devices, extended(): lax.ppermute(tail, axis, [(i, (i + 1) % count) for i in range(ends)])  15.8 us
    ppermute x7, waiting for transfers between devices, extended(): lax.ppermute(head, axis, [((i + 1) % count, i) for i in range(ends)])  15.7 us
    another operation x3, other arithmetic, on_device(): factor = jnp.linalg.cholesky(block)  12.4 us
    another operation x2, other arithmetic, on_device(): current = damping * jax.scipy.linalg.cho_solve((factor, True), rhs_masked)  10.5 us
  transfers between devices with their start and end apart: 15, of which 15 were waited for; matrix products, arithmetic and copies ran while one was open for 0% of the time, Pallas kernels for 0%

commit v1 on v0

v1 whole, which is shorter than its diff:
```python
import functools
import jax
import jax.numpy as jnp
from jax import lax
from jax.experimental import pallas as pl
from jax.experimental.pallas import tpu as pltpu
from jax.sharding import PartitionSpec as P

SWEEPS = 6
DAMPING = 0.7
F32 = jnp.float32
BF16 = jnp.bfloat16
PLANES = 4
CX = 128
SLOTS = 512
CELLS = 512
BLK = 128
COLS = 64
GRP = 4
PANEL = 32
VMEM = pl.BlockSpec(memory_space=pltpu.VMEM)
SMEM = pl.BlockSpec(memory_space=pltpu.SMEM)


def dot(left, right):
    return jnp.dot(left, right, preferred_element_type=F32)


def dot_last(left, right):
    return lax.dot_general(left, right, (((1,), (1,)), ((), ())), preferred_element_type=F32)


def split(values):
    high = values.astype(BF16)
    low = (values - high.astype(F32)).astype(BF16)
    return high, low


def call(kernel, outs, name, scratch=(), limit=16, flops=0, nbytes=0):
    def run(*args):
        specs = [SMEM if a.dtype == jnp.int32 else VMEM for a in args]
        return pl.pallas_call(
            kernel,
            out_shape=[jax.ShapeDtypeStruct(s, d) for s, d in outs],
            in_specs=specs,
            out_specs=[VMEM] * len(outs),
            scratch_shapes=list(scratch),
            name=name,
            cost_estimate=pl.CostEstimate(flops=flops, bytes_accessed=nbytes, transcendentals=0),
            compiler_params=pltpu.CompilerParams(vmem_limit_bytes=limit << 20),
        )(*args)

    return run


def galerkin_kernel(
    info, own, right, left, across0, across1,
    eh_ref, el_ref, blocks_ref, neart_ref, fart_ref, near_ref, far_ref,
    cells, weights, images, square, field,
):
    g = info[0]
    live = info[1]
    even = info[2] == 0
    rows = lax.broadcasted_iota(jnp.int32, (CX, CX), 0)
    cols = lax.broadcasted_iota(jnp.int32, (CX, CX), 1)
    gap = jnp.abs(rows - cols)
    tri = jnp.where(gap == 0, 1.0, jnp.where(gap == 1, 0.5, 0.0)).astype(F32)
    for o in range(GRP):
        for q in range(GRP):
            dist = jnp.abs(lax.rem(g + o, GRP) - lax.rem(g + q, GRP))
            coef = jnp.where(dist == 0, 1.0, jnp.where(dist == 1, 0.5, 0.0)).astype(F32)
            weights[o * CX:(o + 1) * CX, q * CX:(q + 1) * CX] = (tri * coef).astype(BF16)
    for p in range(PLANES):
        for o in range(GRP):
            lanes = slice(p * CELLS + o * CX, p * CELLS + (o + 1) * CX)
            if o == 2:
                plane = across0[p] if p < 2 else across1[p - 2]
            else:
                plane = (own, right, None, left)[o][p]
            cells[:, lanes] = plane[:SLOTS]
            parts = plane[SLOTS:].astype(F32)
            field[p:p + 1, o * CX:(o + 1) * CX] = 16.0 + (parts[0:1] + parts[1:2] + parts[2:3])

    def slot_block(j, carry):
        row = pl.ds(pl.multiple_of(j * BLK, BLK), BLK)
        smooth = []
        for p in range(PLANES):
            smooth.append(dot(cells[row, p * CELLS:(p + 1) * CELLS], weights[...]))
        low_plane, high_plane = smooth[0].astype(BF16), smooth[PLANES - 1].astype(BF16)
        near_ref[row, :] = jnp.where(even, high_plane, low_plane)
        far_ref[row, :] = jnp.where(even, low_plane, high_plane)
        for p in range(PLANES):
            along = smooth[p]
            if p == 0:
                along = along + 0.5 * smooth[1]
            elif p == PLANES - 1:
                along = along + 0.5 * smooth[p - 1]
            else:
                along = along + 0.5 * (smooth[p - 1] + smooth[p + 1])
            own = cells[row, p * CELLS:(p + 1) * CELLS].astype(F32)
            images[:, p * CELLS:(p + 1) * CELLS] = (
                field[p:p + 1, :] * own - 2.0 * along
            ).astype(BF16)
        matrix = dot_last(images[...], cells[...])
        slot = j * BLK + lax.broadcasted_iota(jnp.int32, (BLK, SLOTS), 0)
        column = lax.broadcasted_iota(jnp.int32, (BLK, SLOTS), 1)
        matrix = matrix + jnp.where((slot == column) & (slot >= live), 1.0, 0.0).astype(F32)
        high, low = split(matrix)
        eh_ref[row, :] = high
        el_ref[row, :] = low
        square[...] = matrix
        block = square[:, pl.ds(pl.multiple_of(j * BLK, BLK), BLK)]
        blocks_ref[:, pl.ds(pl.multiple_of(j * BLK, BLK), BLK)] = 0.5 * (block + block.T)
        for c in range(GRP):
            first = (PLANES - 1) * CELLS + c * CX
            low_turned = cells[row, c * CX:(c + 1) * CX].astype(F32).T.astype(BF16)
            high_turned = cells[row, first:first + CX].astype(F32).T.astype(BF16)
            columns = pl.ds(pl.multiple_of(j * BLK, BLK), BLK)
            neart_ref[c * CX:(c + 1) * CX, columns] = jnp.where(even, high_turned, low_turned)
            fart_ref[c * CX:(c + 1) * CX, columns] = jnp.where(even, low_turned, high_turned)
        return carry

    lax.fori_loop(0, GRP, slot_block, 0)


def inverse_kernel(blocks_ref, high_ref, low_ref, work):
    work[...] = blocks_ref[...]
    lane = lax.broadcasted_iota(jnp.int32, (8, BLK), 1)
    sub = lax.broadcasted_iota(jnp.int32, (8, BLK), 0)
    base = lane - lax.rem(lane, PANEL)
    group = lax.div(lane, PANEL)
    within = lax.rem(lane, PANEL)
    group_tall = lax.div(lax.broadcasted_iota(jnp.int32, (BLK, BLK), 1), PANEL)
    count = PANEL // 8
    for p in range(BLK // PANEL):
        rows = slice(p * PANEL, (p + 1) * PANEL)
        packed = None
        for j in range(GRP):
            piece = work[rows, j * BLK:(j + 1) * BLK]
            if j != p:
                piece = pltpu.roll(piece, ((j - p) * PANEL) % BLK, 1)
            packed = piece if packed is None else jnp.where(group_tall[:PANEL] == j, piece, packed)
        tiles = [packed[8 * v:8 * v + 8] for v in range(count)]
        for k in range(0, PANEL, 2):
            v, q = k // 8, k % 8
            col0 = [jnp.take_along_axis(t, base + k, axis=1) for t in tiles]
            col1 = [jnp.take_along_axis(t, base + (k + 1), axis=1) for t in tiles]
            spread = lambda t, i: jnp.broadcast_to(t[i:i + 1], (8, BLK))
            row0, row1 = spread(tiles[v], q), spread(tiles[v], q + 1)
            p00, p10 = spread(col0[v], q), spread(col0[v], q + 1)
            p01, p11 = spread(col1[v], q), spread(col1[v], q + 1)
            scale = 1.0 / (p00 * p11 - p01 * p10)
            is0, is1 = within == k, within == k + 1
            row0 = jnp.where(is0, 1.0, jnp.where(is1, 0.0, row0))
            row1 = jnp.where(is0, 0.0, jnp.where(is1, 1.0, row1))
            new0 = (p11 * scale) * row0 - (p01 * scale) * row1
            new1 = (p00 * scale) * row1 - (p10 * scale) * row0
            for u in range(count):
                tile = jnp.where(is0 | is1, 0.0, tiles[u]) - col0[u] * new0 - col1[u] * new1
                if u == v:
                    tile = jnp.where(sub == q, new0, jnp.where(sub == q + 1, new1, tile))
                tiles[u] = tile
        packed = jnp.concatenate(tiles, axis=0)
        for j in range(GRP):
            lanes = slice(j * BLK, (j + 1) * BLK)
            block = work[:, lanes]
            pivot = pltpu.roll(packed, (-j * PANEL) % BLK, 1) if j else packed
            spot = pltpu.roll(packed, ((p - j) * PANEL) % BLK, 1) if j != p else packed
            tall = pltpu.roll(block, (-p * PANEL) % BLK, 1) if p else block
            mult = jnp.dot(
                pivot[:, :PANEL], block[rows], preferred_element_type=F32,
                precision=lax.Precision.HIGHEST,
            )
            mult = jnp.where(group_tall[:PANEL] == p, spot, mult)
            change = jnp.dot(
                tall[:, :PANEL], mult, preferred_element_type=F32,
                precision=lax.Precision.HIGHEST,
            )
            work[:, lanes] = jnp.where(group_tall == p, 0.0, block) - change
            work[rows, lanes] = mult
    high, low = split(work[...])
    high_ref[...] = high
    low_ref[...] = low


def precondition(residual, ih_ref, il_ref):
    parts = []
    for j in range(GRP):
        lanes = slice(j * BLK, (j + 1) * BLK)
        high, low = split(residual[:, lanes])
        both = dot(jnp.concatenate([high, low], axis=0), ih_ref[:, lanes])
        parts.append(both[:COLS] + both[COLS:] + dot(high, il_ref[:, lanes]))
    return DAMPING * jnp.concatenate(parts, axis=1)


def first_kernel(r_ref, ih_ref, il_ref, near_ref, far_ref, d_ref, near_out, far_out):
    delta = precondition(r_ref[...], ih_ref, il_ref)
    d_ref[...] = delta
    sent = delta.astype(BF16)
    far_out[...] = dot(sent, far_ref[...]).astype(BF16)
    near_out[...] = dot(sent, near_ref[...]).astype(BF16)


def local_kernel(r_ref, d_ref, eh_ref, el_ref, t_ref):
    high, low = split(d_ref[...])
    both = dot(jnp.concatenate([high, low], axis=0), eh_ref[...])
    t_ref[...] = r_ref[...] - (both[:COLS] + both[COLS:] + dot(high, el_ref[...]))


def sweep_kernel(
    t_ref, x_ref, far_in, near_in, neart_ref, fart_ref, ih_ref, il_ref, near_ref, far_ref,
    r_ref, d_ref, new_ref, near_out, far_out,
):
    residual = t_ref[...] + dot(near_in[...], neart_ref[...]) + dot(far_in[...], fart_ref[...])
    r_ref[...] = residual
    delta = precondition(residual, ih_ref, il_ref)
    d_ref[...] = delta
    new_ref[...] = x_ref[...] + delta
    sent = delta.astype(BF16)
    far_out[...] = dot(sent, far_ref[...]).astype(BF16)
    near_out[...] = dot(sent, near_ref[...]).astype(BF16)


def last_kernel(t_ref, x_ref, far_in, near_in, neart_ref, fart_ref, ih_ref, il_ref, out_ref):
    residual = t_ref[...] + dot(near_in[...], neart_ref[...]) + dot(far_in[...], fart_ref[...])
    out_ref[...] = x_ref[...] + precondition(residual, ih_ref, il_ref)


def shift_by(values, offset):
    return lax.ppermute(values, "grp", [(i, (i + offset) % GRP) for i in range(GRP)])


def on_device(deflation, shift_field, counts, right_sides):
    g = lax.axis_index("grp")
    subs = lax.axis_size("sub")
    live_count = counts[0]
    parity = lax.rem(lax.axis_index("sub"), 2)
    info = jnp.stack([g.astype(jnp.int32), live_count, parity.astype(jnp.int32)])
    slot_ids = lax.iota(jnp.int32, SLOTS)
    live = slot_ids < live_count
    masked = jnp.where(live[:, None, None, None], deflation, jnp.zeros((), BF16))
    planes = jnp.transpose(masked.reshape(SLOTS, PLANES, CX), (1, 0, 2))
    part0 = shift_field.astype(BF16)
    rest = shift_field - part0.astype(F32)
    part1 = rest.astype(BF16)
    part2 = (rest - part1.astype(F32)).astype(BF16)
    extra = jnp.concatenate([part0, part1, part2, jnp.zeros((PLANES, 13, CX), BF16)], axis=1)
    own = jnp.concatenate([planes, extra], axis=1)
    row_slot = g * BLK + lax.iota(jnp.int32, BLK)
    rhs = jnp.where((row_slot >= live_count)[:, None], 0.0, right_sides).T
    left = shift_by(own, 1)
    right = shift_by(own, -1)
    start = lax.all_to_all(rhs, "grp", 0, 1, tiled=True)
    across0 = shift_by(left[:2], 1)
    across1 = shift_by(right[2:], -1)

    square = (SLOTS, SLOTS)
    eh, el, blocks, neart, fart, near, far = call(
        galerkin_kernel,
        [(square, BF16), (square, BF16), ((BLK, SLOTS), F32)] + [(square, BF16)] * 4,
        "galerkin",
        scratch=[
            pltpu.VMEM((SLOTS, PLANES * CELLS), BF16),
            pltpu.VMEM((CELLS, CELLS), BF16),
            pltpu.VMEM((BLK, PLANES * CELLS), BF16),
            pltpu.VMEM((BLK, SLOTS), F32),
            pltpu.VMEM((8, CELLS), F32),
        ],
        limit=24,
        flops=2 * 10**9,
        nbytes=6 << 20,
    )(info, own, right, left, across0, across1)
    ih, il = call(
        inverse_kernel,
        [((BLK, SLOTS), BF16)] * 2,
        "inverse",
        scratch=[pltpu.VMEM((BLK, SLOTS), F32)],
        flops=10**9,
        nbytes=1 << 19,
    )(blocks)

    vec = (COLS, SLOTS)
    r = start
    d, near_msg, far_msg = call(
        first_kernel, [(vec, F32), (vec, BF16), (vec, BF16)], "first",
        flops=10**8, nbytes=2 << 20,
    )(r, ih, il, near, far)
    x = d
    near_pairs = [(i, i ^ 1) for i in range(subs)]
    far_pairs = [(i, ((i + 1) ^ 1) - 1) for i in range(1, subs - 1)]
    for sweep in range(1, SWEEPS):
        far_got = lax.ppermute(far_msg, "sub", far_pairs)
        near_got = lax.ppermute(near_msg, "sub", near_pairs)
        (t,) = call(local_kernel, [(vec, F32)], "local", flops=10**8, nbytes=1 << 20)(r, d, eh, el)
        if sweep < SWEEPS - 1:
            r, d, x, near_msg, far_msg = call(
                sweep_kernel,
                [(vec, F32), (vec, F32), (vec, F32), (vec, BF16), (vec, BF16)],
                "sweep", flops=2 * 10**8, nbytes=3 << 20,
            )(t, x, far_got, near_got, neart, fart, ih, il, near, far)
        else:
            (x,) = call(
                last_kernel, [(vec, F32)], "last", flops=10**8, nbytes=2 << 20,
            )(t, x, far_got, near_got, neart, fart, ih, il)
    return lax.all_to_all(x, "grp", 1, 0, tiled=True).T


def solution(mesh):
    in_specs = (
        P(None, "sub", "grp", None),
        P("sub", "grp", None),
        P("sub"),
        P(("sub", "grp"), None),
    )
    return jax.shard_map(
        on_device, mesh=mesh, in_specs=in_specs,
        out_specs=P(("sub", "grp"), None), check_vma=False,
    )
```

time: 335 us -> 110 us (0.33)
  waiting for transfers between devices: 140 us -> 15 us
  blocking collectives: 65.2 us -> 10.7 us
  other arithmetic: 34.3 us -> 1.94 us
  Pallas kernels: 0 us -> 21.1 us
  between operations: 14.5 us -> 0.99 us
  matrix products: 12.5 us -> 0 us
  starting transfers between devices: 62.4 us -> 58 us
  local copies, waits for them, and re-layouts: 5.69 us -> 1.93 us
    psum x1 -> x0, waiting for transfers between devices: 88.7 us -> none  [on_device(): lax.psum(jnp.concatenate([lower_part, middle, upper_part], axis=1), 'grp')]
    all_gather x5 -> x0, blocking collectives: 65.2 us -> none  [on_device(): slab_iter = lax.all_gather(current, 'grp', axis=0, tiled=True)]
    ppermute x14, waiting for transfers between devices: 51.5 us -> 15 us  [the longest x4 10.4 us: shift_by(): lax.ppermute(values, 'grp', [(i, (i + offset) % GRP) for i in range(GRP)])]
    another operation x6 -> x1, other arithmetic: 23.1 us -> 0.08 us  [on_device(): jnp.stack([g.astype(jnp.int32), live_count, parity.astype(jnp.int32)])]
    pallas_call x0 -> x13, Pallas kernels: none -> 21.1 us  [run(): pl.pallas_call(kernel, out_shape=[jax.ShapeDtypeStruct(s, d) for s, d in...]
    all_to_all x0 -> x1, blocking collectives: none -> 10.7 us  [on_device(): return lax.all_to_all(x, 'grp', 1, 0, tiled=True).T]
    dot_general x8 -> x0, matrix products: 8.36 us -> none  [the longest x5 7.28 us: on_device(): product = jnp.dot(matrix, stacked, precision=lax.Precision.HIGHEST)]
    ppermute x14, starting transfers between devices: 62.3 us -> 54.7 us  [the longest x5 30.9 us: on_device(): far_got = lax.ppermute(far_msg, 'sub', far_pairs)]
  transfers between devices with their start and end apart: 15 -> 15, of which waited for: 15 -> 8; matrix products, arithmetic and copies ran while one was open for 0% -> 1% of each run, Pallas kernels for 0% -> 1%
where the time goes in v1:
time: 110 us
  starting transfers between devices  58 us (53%)
  Pallas kernels  21.1 us (19%)
  waiting for transfers between devices  15 us (14%)
  blocking collectives  10.7 us (10%)
  other arithmetic  1.94 us (2%)
  local copies, waits for them, and re-layouts  1.93 us (2%)
    ppermute x5, starting transfers between devices, on_device(): far_got = lax.ppermute(far_msg, 'sub', far_pairs)  30.9 us
    pallas_call x13, Pallas kernels, run(): pl.pallas_call(kernel, out_shape=[jax.ShapeDtypeStruct(s, d) for s, d in...  21.1 us
    ppermute x4, starting transfers between devices, shift_by(): lax.ppermute(values, 'grp', [(i, (i + offset) % GRP) for i in range(GRP)])  14.1 us
    all_to_all x1, blocking collectives, on_device(): return lax.all_to_all(x, 'grp', 1, 0, tiled=True).T  10.7 us
    ppermute x4, waiting for transfers between devices, shift_by(): lax.ppermute(values, 'grp', [(i, (i + offset) % GRP) for i in range(GRP)])  10.4 us
    ppermute x5, starting transfers between devices, on_device(): near_got = lax.ppermute(near_msg, 'sub', near_pairs)  9.6 us
    ppermute x5, waiting for transfers between devices, on_device(): far_got = lax.ppermute(far_msg, 'sub', far_pairs)  3.68 us
    all_to_all x1, starting transfers between devices, on_device(): start = lax.all_to_all(rhs, 'grp', 0, 1, tiled=True)  3.33 us
  transfers between devices with their start and end apart: 15, of which 8 were waited for; matrix products, arithmetic and copies ran while one was open for 1% of the time, Pallas kernels for 1%

profile of v1, /device:TPU:32, one launch (start us, length us, event | category | flops | bytes accessed | tf_op | source)
XLA Modules:
  0.0 109.7 jit_solution(11171243893531164822)
XLA Ops:
  0.7 0.0 copy-start.1
  0.7 0.7 copy-done.1
  1.3 1.2 %fusion = bf16[4,512,128]{2,1,0:T(8,128)(2,1)S(1)} fusion(bf16[512,4,1,128]{3,1,2,0:T(4,128)(2,1)} %param.4, pred[512]{0:T(512)(128)(4,1)S(1)} %iota_compare_fusion), kind=kLoop, calls=%fused_computation.1 | loop fusion | flops 262144 | bytes 1049088 | tf_op jit(solution)/shard_map/transpose | solution.py:242
  2.5 0.0 copy-start
  2.5 0.4 concatenate.3.own
  2.9 3.4 %collective-permute-start.1 = (bf16[4,528,128]{2,1,0:T(8,128)(2,1)S(1)}, bf16[4,528,128]{2,1,0:T(8,128)(2,1)S(1)}, u32[]{:S(2)}, u32[]{:S(2)}) collective-permute-start(bf16[4,528,128]{2,1,0:T(8,128)(2,1)S(1)} %concatenate.3.own), channel_id=1, source_target_pairs={{0,1},{1,2},{2,3},{3,0},{4,5},{5,6},{6,7},{7,4},{8,9},{9,10},{10,1... | collective-permute-start | bytes 1622024 | tf_op jit(solution)/shard_map/ppermute | solution.py:230
  6.3 3.7 %collective-permute-start = (bf16[4,528,128]{2,1,0:T(8,128)(2,1)S(1)}, bf16[4,528,128]{2,1,0:T(8,128)(2,1)S(1)}, u32[]{:S(2)}, u32[]{:S(2)}) collective-permute-start(bf16[4,528,128]{2,1,0:T(8,128)(2,1)S(1)} %concatenate.3.own), channel_id=1, source_target_pairs={{0,3},{1,0},{2,1},{3,2},{4,7},{5,4},{6,5},{7,6},{8,11},{9,8},{10,9... | collective-permute-start | bytes 1622024 | tf_op jit(solution)/shard_map/ppermute | solution.py:230
  10.0 0.0 copy-done
  10.0 0.1 copy.8
  10.1 0.7 broadcast_select_fusion
  10.8 3.3 %all-to-all-start = ((f32[4,64,128]{2,1,0:T(8,128)}), f32[4,64,128]{2,1,0:T(8,128)S(1)}, u32[]{:S(2)}, u32[]{:S(2)}) async-start(f32[4,64,128]{2,1,0:T(8,128)} %bitcast.2), calls=%async_computation | async-start | bytes 262144 | tf_op jit(solution)/shard_map/all_to_all | solution.py:253
  14.1 6.3 %collective-permute-done.1.left = bf16[4,528,128]{2,1,0:T(8,128)(2,1)S(1)} collective-permute-done((bf16[4,528,128]{2,1,0:T(8,128)(2,1)S(1)}, bf16[4,528,128]{2,1,0:T(8,128)(2,1)S(1)}, u32[]{:S(2)}, u32[]{:S(2)}) %collective-permute-start.1) | collective-permute-done | bytes 540704 | tf_op jit(solution)/shard_map/ppermute | solution.py:230
  20.4 2.5 %collective-permute-start.2 = (bf16[2,528,128]{2,1,0:T(8,128)(2,1)S(1)}, bf16[2,528,128]{2,1,0:T(8,128)(2,1)S(1)}, u32[]{:S(2)}, u32[]{:S(2)}) collective-permute-start(bf16[2,528,128]{2,1,0:T(8,128)(2,1)S(1)} %slice.8), channel_id=1, source_target_pairs={{0,1},{1,2},{2,3},{3,0},{4,5},{5,6},{6,7},{7,4},{8,9},{9,10},{10,1... | collective-permute-start | bytes 811016 | tf_op jit(solution)/shard_map/ppermute | solution.py:230
  23.0 0.0 collective-permute-done.right
  23.0 4.5 %collective-permute-start.3 = (bf16[2,528,128]{2,1,0:T(8,128)(2,1)S(1)}, bf16[2,528,128]{2,1,0:T(8,128)(2,1)S(1)}, u32[]{:S(2)}, u32[]{:S(2)}) collective-permute-start(bf16[2,528,128]{2,1,0:T(8,128)(2,1)S(1)} %slice.9), channel_id=1, source_target_pairs={{0,3},{1,0},{2,1},{3,2},{4,7},{5,4},{6,5},{7,6},{8,11},{9,8},{10,9... | collective-permute-start | bytes 811016 | tf_op jit(solution)/shard_map/ppermute | solution.py:230
  27.5 0.1 pad_add_fusion.info
  27.6 0.0 all-to-all-done
  27.6 2.9 %collective-permute-done.2.across0 = bf16[2,528,128]{2,1,0:T(8,128)(2,1)S(1)} collective-permute-done((bf16[2,528,128]{2,1,0:T(8,128)(2,1)S(1)}, bf16[2,528,128]{2,1,0:T(8,128)(2,1)S(1)}, u32[]{:S(2)}, u32[]{:S(2)}) %collective-permute-start.2) | collective-permute-done | bytes 270368 | tf_op jit(solution)/shard_map/ppermute | solution.py:230
  30.5 1.2 %collective-permute-done.3.across1 = bf16[2,528,128]{2,1,0:T(8,128)(2,1)S(1)} collective-permute-done((bf16[2,528,128]{2,1,0:T(8,128)(2,1)S(1)}, bf16[2,528,128]{2,1,0:T(8,128)(2,1)S(1)}, u32[]{:S(2)}, u32[]{:S(2)}) %collective-permute-start.3) | collective-permute-done | bytes 270368 | tf_op jit(solution)/shard_map/ppermute | solution.py:230
  31.7 6.7 %galerkin.1 = (bf16[512,512]{1,0:T(8,128)(2,1)S(1)}, bf16[512,512]{1,0:T(8,128)(2,1)S(1)}, f32[128,512]{1,0:T(8,128)S(1)}, bf16[512,512]{1,0:T(8,128)(2,1)S(1)},...) custom-call(s32[3]{0:T(128)S(1)} %pad_add_fusion.info, ...), custom_call_target="tpu_custom_call" | custom-call | flops 2000000000 | bytes 6291456 | tf_op jit(solution)/shard_map/galerkin/pallas_call | solution.py:42
  38.5 9.2 %inverse.1 = (bf16[128,512]{1,0:T(8,128)(2,1)S(1)}, bf16[128,512]{1,0:T(8,128)(2,1)S(1)}) custom-call(f32[128,512]{1,0:T(8,128)S(1)} %get-tuple-element.37.blocks_ref), custom_call_target="tpu_custom_call" | custom-call | flops 1000000000 | bytes 524288 | tf_op jit(solution)/shard_map/inverse/pallas_call | solution.py:42
  47.7 0.4 first.1
  48.2 7.9 %collective-permute-start.4 = (bf16[64,512]{1,0:T(8,128)(2,1)S(1)}, bf16[64,512]{1,0:T(8,128)(2,1)S(1)}, u32[]{:S(2)}, u32[]{:S(2)}) collective-permute-start(bf16[64,512]{1,0:T(8,128)(2,1)S(1)} %get-tuple-element.45), channel_id=1, source_target_pairs={{4,8},{8,4},{12,16},{16,12},{20,24},{24,20},{28,32},{32,28},{36,40... | collective-permute-start | bytes 196616 | tf_op jit(solution)/shard_map/ppermute | solution.py:292
  56.1 1.9 %collective-permute-start.5 = (bf16[64,512]{1,0:T(8,128)(2,1)S(1)}, bf16[64,512]{1,0:T(8,128)(2,1)S(1)}, u32[]{:S(2)}, u32[]{:S(2)}) collective-permute-start(bf16[64,512]{1,0:T(8,128)(2,1)S(1)} %get-tuple-element.46), channel_id=1, source_target_pairs={{0,4},{4,0},{8,12},{12,8},{16,20},{20,16},{24,28},{28,24},{32,36},... | collective-permute-start | bytes 196616 | tf_op jit(solution)/shard_map/ppermute | solution.py:293
  58.0 0.3 local.5.t_ref
  58.3 0.0 collective-permute-done.4.far_in
  58.3 0.9 collective-permute-done.5.near_in
  59.2 0.7 sweep.4
  59.9 5.8 %collective-permute-start.6 = (bf16[64,512]{1,0:T(8,128)(2,1)S(1)}, bf16[64,512]{1,0:T(8,128)(2,1)S(1)}, u32[]{:S(2)}, u32[]{:S(2)}) collective-permute-start(bf16[64,512]{1,0:T(8,128)(2,1)S(1)} %get-tuple-element.52), channel_id=1, source_target_pairs={{4,8},{8,4},{12,16},{16,12},{20,24},{24,20},{28,32},{32,28},{36,40... | collective-permute-start | bytes 196616 | tf_op jit(solution)/shard_map/ppermute | solution.py:292
  65.7 1.9 %collective-permute-start.7 = (bf16[64,512]{1,0:T(8,128)(2,1)S(1)}, bf16[64,512]{1,0:T(8,128)(2,1)S(1)}, u32[]{:S(2)}, u32[]{:S(2)}) collective-permute-start(bf16[64,512]{1,0:T(8,128)(2,1)S(1)} %get-tuple-element.53), channel_id=1, source_target_pairs={{0,4},{4,0},{8,12},{12,8},{16,20},{20,16},{24,28},{28,24},{32,36},... | collective-permute-start | bytes 196616 | tf_op jit(solution)/shard_map/ppermute | solution.py:293
  67.6 0.3 local.6.t_ref
  67.9 0.9 collective-permute-done.6.far_in
  68.8 0.0 collective-permute-done.7.near_in
  68.8 0.7 sweep.5
  69.6 5.8 %collective-permute-start.8 = (bf16[64,512]{1,0:T(8,128)(2,1)S(1)}, bf16[64,512]{1,0:T(8,128)(2,1)S(1)}, u32[]{:S(2)}, u32[]{:S(2)}) collective-permute-start(bf16[64,512]{1,0:T(8,128)(2,1)S(1)} %get-tuple-element.57), channel_id=1, source_target_pairs={{4,8},{8,4},{12,16},{16,12},{20,24},{24,20},{28,32},{32,28},{36,40... | collective-permute-start | bytes 196616 | tf_op jit(solution)/shard_map/ppermute | solution.py:292
  75.3 1.9 %collective-permute-start.9 = (bf16[64,512]{1,0:T(8,128)(2,1)S(1)}, bf16[64,512]{1,0:T(8,128)(2,1)S(1)}, u32[]{:S(2)}, u32[]{:S(2)}) collective-permute-start(bf16[64,512]{1,0:T(8,128)(2,1)S(1)} %get-tuple-element.58), channel_id=1, source_target_pairs={{0,4},{4,0},{8,12},{12,8},{16,20},{20,16},{24,28},{28,24},{32,36},... | collective-permute-start | bytes 196616 | tf_op jit(solution)/shard_map/ppermute | solution.py:293
  77.3 0.3 local.7.t_ref
  77.5 0.9 collective-permute-done.8.far_in
  78.5 0.0 collective-permute-done.9.near_in
  78.5 0.7 sweep.6
  79.2 5.8 %collective-permute-start.10 = (bf16[64,512]{1,0:T(8,128)(2,1)S(1)}, bf16[64,512]{1,0:T(8,128)(2,1)S(1)}, u32[]{:S(2)}, u32[]{:S(2)}) collective-permute-start(bf16[64,512]{1,0:T(8,128)(2,1)S(1)} %get-tuple-element.62), channel_id=1, source_target_pairs={{4,8},{8,4},{12,16},{16,12},{20,24},{24,20},{28,32},{32,28},{36,40... | collective-permute-start | bytes 196616 | tf_op jit(solution)/shard_map/ppermute | solution.py:292
  84.9 1.9 %collective-permute-start.11 = (bf16[64,512]{1,0:T(8,128)(2,1)S(1)}, bf16[64,512]{1,0:T(8,128)(2,1)S(1)}, u32[]{:S(2)}, u32[]{:S(2)}) collective-permute-start(bf16[64,512]{1,0:T(8,128)(2,1)S(1)} %get-tuple-element.63), channel_id=1, source_target_pairs={{0,4},{4,0},{8,12},{12,8},{16,20},{20,16},{24,28},{28,24},{32,36},... | collective-permute-start | bytes 196616 | tf_op jit(solution)/shard_map/ppermute | solution.py:293
  86.9 0.3 local.8.t_ref
  87.2 0.9 collective-permute-done.10.far_in
  88.1 0.0 collective-permute-done.11.near_in
  88.1 0.7 sweep.7
  88.8 5.8 %collective-permute-start.12 = (bf16[64,512]{1,0:T(8,128)(2,1)S(1)}, bf16[64,512]{1,0:T(8,128)(2,1)S(1)}, u32[]{:S(2)}, u32[]{:S(2)}) collective-permute-start(bf16[64,512]{1,0:T(8,128)(2,1)S(1)} %get-tuple-element.67), channel_id=1, source_target_pairs={{4,8},{8,4},{12,16},{16,12},{20,24},{24,20},{28,32},{32,28},{36,40... | collective-permute-start | bytes 196616 | tf_op jit(solution)/shard_map/ppermute | solution.py:292
  94.6 1.9 %collective-permute-start.13 = (bf16[64,512]{1,0:T(8,128)(2,1)S(1)}, bf16[64,512]{1,0:T(8,128)(2,1)S(1)}, u32[]{:S(2)}, u32[]{:S(2)}) collective-permute-start(bf16[64,512]{1,0:T(8,128)(2,1)S(1)} %get-tuple-element.68), channel_id=1, source_target_pairs={{0,4},{4,0},{8,12},{12,8},{16,20},{20,16},{24,28},{28,24},{32,36},... | collective-permute-start | bytes 196616 | tf_op jit(solution)/shard_map/ppermute | solution.py:293
  96.5 0.3 local.9.t_ref
  96.8 0.9 collective-permute-done.12.far_in
  97.7 0.0 collective-permute-done.13.near_in
  97.7 0.5 last.1
  98.2 10.7 %all_to_all.38 = f32[64,4,128]{2,0,1:T(8,128)S(1)} all-to-all(f32[64,4,128]{2,0,1:T(8,128)S(1)} %copy_bitcast_fusion.1), channel_id=1, replica_groups=mesh['sub'=128,'grp'=4] {'grp'}, dimensions={1} | all-to-all | bytes 262144 | tf_op jit(solution)/shard_map/all_to_all | solution.py:305
  108.9 0.8 copy.12
  (8 shorter events, 0.1 us)
Async XLA Ops:
  0.7 0.7 copy-start.1
  2.5 7.5 %copy-start = (f32[128,256]{1,0:T(8,128)S(1)}, f32[128,256]{1,0:T(8,128)}, u32[]{:S(2)}) copy-start(f32[128,256]{1,0:T(8,128)} %param.7) | copy-start | bytes 393220
  2.9 17.5 %collective-permute-start.1 = (bf16[4,528,128]{2,1,0:T(8,128)(2,1)S(1)}, bf16[4,528,128]{2,1,0:T(8,128)(2,1)S(1)}, u32[]{:S(2)}, u32[]{:S(2)}) collective-permute-start(bf16[4,528,128]{2,1,0:T(8,128)(2,1)S(1)} %concatenate.3.own), channel_id=1, source_target_pairs={{0,1},{1,2},{2,3},{3,0},{4,5},{5,6},{6,7},{7,4},{8,9},{9,10},{10,1... | collective-permute-start | bytes 1622024 | tf_op jit(solution)/shard_map/ppermute | solution.py:230
  6.3 16.6 %collective-permute-start = (bf16[4,528,128]{2,1,0:T(8,128)(2,1)S(1)}, bf16[4,528,128]{2,1,0:T(8,128)(2,1)S(1)}, u32[]{:S(2)}, u32[]{:S(2)}) collective-permute-start(bf16[4,528,128]{2,1,0:T(8,128)(2,1)S(1)} %concatenate.3.own), channel_id=1, source_target_pairs={{0,3},{1,0},{2,1},{3,2},{4,7},{5,4},{6,5},{7,6},{8,11},{9,8},{10,9... | collective-permute-start | bytes 1622024 | tf_op jit(solution)/shard_map/ppermute | solution.py:230
  10.8 16.9 %all-to-all-start = ((f32[4,64,128]{2,1,0:T(8,128)}), f32[4,64,128]{2,1,0:T(8,128)S(1)}, u32[]{:S(2)}, u32[]{:S(2)}) async-start(f32[4,64,128]{2,1,0:T(8,128)} %bitcast.2), calls=%async_computation | async-start | bytes 262144 | tf_op jit(solution)/shard_map/all_to_all | solution.py:253
  20.4 10.1 %collective-permute-start.2 = (bf16[2,528,128]{2,1,0:T(8,128)(2,1)S(1)}, bf16[2,528,128]{2,1,0:T(8,128)(2,1)S(1)}, u32[]{:S(2)}, u32[]{:S(2)}) collective-permute-start(bf16[2,528,128]{2,1,0:T(8,128)(2,1)S(1)} %slice.8), channel_id=1, source_target_pairs={{0,1},{1,2},{2,3},{3,0},{4,5},{5,6},{6,7},{7,4},{8,9},{9,10},{10,1... | collective-permute-start | bytes 811016 | tf_op jit(solution)/shard_map/ppermute | solution.py:230
  23.0 8.8 %collective-permute-start.3 = (bf16[2,528,128]{2,1,0:T(8,128)(2,1)S(1)}, bf16[2,528,128]{2,1,0:T(8,128)(2,1)S(1)}, u32[]{:S(2)}, u32[]{:S(2)}) collective-permute-start(bf16[2,528,128]{2,1,0:T(8,128)(2,1)S(1)} %slice.9), channel_id=1, source_target_pairs={{0,3},{1,0},{2,1},{3,2},{4,7},{5,4},{6,5},{7,6},{8,11},{9,8},{10,9... | collective-permute-start | bytes 811016 | tf_op jit(solution)/shard_map/ppermute | solution.py:230
  48.2 10.2 %collective-permute-start.4 = (bf16[64,512]{1,0:T(8,128)(2,1)S(1)}, bf16[64,512]{1,0:T(8,128)(2,1)S(1)}, u32[]{:S(2)}, u32[]{:S(2)}) collective-permute-start(bf16[64,512]{1,0:T(8,128)(2,1)S(1)} %get-tuple-element.45), channel_id=1, source_target_pairs={{4,8},{8,4},{12,16},{16,12},{20,24},{24,20},{28,32},{32,28},{36,40... | collective-permute-start | bytes 196616 | tf_op jit(solution)/shard_map/ppermute | solution.py:292
  56.1 3.1 %collective-permute-start.5 = (bf16[64,512]{1,0:T(8,128)(2,1)S(1)}, bf16[64,512]{1,0:T(8,128)(2,1)S(1)}, u32[]{:S(2)}, u32[]{:S(2)}) collective-permute-start(bf16[64,512]{1,0:T(8,128)(2,1)S(1)} %get-tuple-element.46), channel_id=1, source_target_pairs={{0,4},{4,0},{8,12},{12,8},{16,20},{20,16},{24,28},{28,24},{32,36},... | collective-permute-start | bytes 196616 | tf_op jit(solution)/shard_map/ppermute | solution.py:293
  59.9 8.9 %collective-permute-start.6 = (bf16[64,512]{1,0:T(8,128)(2,1)S(1)}, bf16[64,512]{1,0:T(8,128)(2,1)S(1)}, u32[]{:S(2)}, u32[]{:S(2)}) collective-permute-start(bf16[64,512]{1,0:T(8,128)(2,1)S(1)} %get-tuple-element.52), channel_id=1, source_target_pairs={{4,8},{8,4},{12,16},{16,12},{20,24},{24,20},{28,32},{32,28},{36,40... | collective-permute-start | bytes 196616 | tf_op jit(solution)/shard_map/ppermute | solution.py:292
  65.7 3.1 %collective-permute-start.7 = (bf16[64,512]{1,0:T(8,128)(2,1)S(1)}, bf16[64,512]{1,0:T(8,128)(2,1)S(1)}, u32[]{:S(2)}, u32[]{:S(2)}) collective-permute-start(bf16[64,512]{1,0:T(8,128)(2,1)S(1)} %get-tuple-element.53), channel_id=1, source_target_pairs={{0,4},{4,0},{8,12},{12,8},{16,20},{20,16},{24,28},{28,24},{32,36},... | collective-permute-start | bytes 196616 | tf_op jit(solution)/shard_map/ppermute | solution.py:293
  69.6 8.9 %collective-permute-start.8 = (bf16[64,512]{1,0:T(8,128)(2,1)S(1)}, bf16[64,512]{1,0:T(8,128)(2,1)S(1)}, u32[]{:S(2)}, u32[]{:S(2)}) collective-permute-start(bf16[64,512]{1,0:T(8,128)(2,1)S(1)} %get-tuple-element.57), channel_id=1, source_target_pairs={{4,8},{8,4},{12,16},{16,12},{20,24},{24,20},{28,32},{32,28},{36,40... | collective-permute-start | bytes 196616 | tf_op jit(solution)/shard_map/ppermute | solution.py:292
  75.3 3.1 %collective-permute-start.9 = (bf16[64,512]{1,0:T(8,128)(2,1)S(1)}, bf16[64,512]{1,0:T(8,128)(2,1)S(1)}, u32[]{:S(2)}, u32[]{:S(2)}) collective-permute-start(bf16[64,512]{1,0:T(8,128)(2,1)S(1)} %get-tuple-element.58), channel_id=1, source_target_pairs={{0,4},{4,0},{8,12},{12,8},{16,20},{20,16},{24,28},{28,24},{32,36},... | collective-permute-start | bytes 196616 | tf_op jit(solution)/shard_map/ppermute | solution.py:293
  79.2 8.9 %collective-permute-start.10 = (bf16[64,512]{1,0:T(8,128)(2,1)S(1)}, bf16[64,512]{1,0:T(8,128)(2,1)S(1)}, u32[]{:S(2)}, u32[]{:S(2)}) collective-permute-start(bf16[64,512]{1,0:T(8,128)(2,1)S(1)} %get-tuple-element.62), channel_id=1, source_target_pairs={{4,8},{8,4},{12,16},{16,12},{20,24},{24,20},{28,32},{32,28},{36,40... | collective-permute-start | bytes 196616 | tf_op jit(solution)/shard_map/ppermute | solution.py:292
  84.9 3.1 %collective-permute-start.11 = (bf16[64,512]{1,0:T(8,128)(2,1)S(1)}, bf16[64,512]{1,0:T(8,128)(2,1)S(1)}, u32[]{:S(2)}, u32[]{:S(2)}) collective-permute-start(bf16[64,512]{1,0:T(8,128)(2,1)S(1)} %get-tuple-element.63), channel_id=1, source_target_pairs={{0,4},{4,0},{8,12},{12,8},{16,20},{20,16},{24,28},{28,24},{32,36},... | collective-permute-start | bytes 196616 | tf_op jit(solution)/shard_map/ppermute | solution.py:293
  88.8 8.9 %collective-permute-start.12 = (bf16[64,512]{1,0:T(8,128)(2,1)S(1)}, bf16[64,512]{1,0:T(8,128)(2,1)S(1)}, u32[]{:S(2)}, u32[]{:S(2)}) collective-permute-start(bf16[64,512]{1,0:T(8,128)(2,1)S(1)} %get-tuple-element.67), channel_id=1, source_target_pairs={{4,8},{8,4},{12,16},{16,12},{20,24},{24,20},{28,32},{32,28},{36,40... | collective-permute-start | bytes 196616 | tf_op jit(solution)/shard_map/ppermute | solution.py:292
  94.6 3.1 %collective-permute-start.13 = (bf16[64,512]{1,0:T(8,128)(2,1)S(1)}, bf16[64,512]{1,0:T(8,128)(2,1)S(1)}, u32[]{:S(2)}, u32[]{:S(2)}) collective-permute-start(bf16[64,512]{1,0:T(8,128)(2,1)S(1)} %get-tuple-element.68), channel_id=1, source_target_pairs={{0,4},{4,0},{8,12},{12,8},{16,20},{20,16},{24,28},{28,24},{32,36},... | collective-permute-start | bytes 196616 | tf_op jit(solution)/shard_map/ppermute | solution.py:293

commit v2 on v1

v2 whole, which is shorter than its diff:
```python
import jax
import jax.numpy as jnp
from jax import lax
from jax.experimental import pallas as pl
from jax.experimental.pallas import tpu as pltpu
from jax.sharding import PartitionSpec as P

SWEEPS = 6
DAMPING = 0.7
F32 = jnp.float32
BF16 = jnp.bfloat16
PLANES = 4
CX = 128
SLOTS = 512
HALF = 256
CELLS = 512
BLK = 128
COLS = 64
GRP = 4
PANEL = 32
VMEM = pl.BlockSpec(memory_space=pltpu.VMEM)
SMEM = pl.BlockSpec(memory_space=pltpu.SMEM)


def dot(left, right):
    return jnp.dot(left, right, preferred_element_type=F32)


def dot_last(left, right):
    return lax.dot_general(left, right, (((1,), (1,)), ((), ())), preferred_element_type=F32)


def split(values):
    high = values.astype(BF16)
    low = (values - high.astype(F32)).astype(BF16)
    return high, low


def call(kernel, outs, scratch=(), limit=16, flops=0, nbytes=0):
    def run(*args):
        specs = [SMEM if a.dtype == jnp.int32 else VMEM for a in args]
        return pl.pallas_call(
            kernel,
            out_shape=[jax.ShapeDtypeStruct(s, d) for s, d in outs],
            in_specs=specs,
            out_specs=[VMEM] * len(outs),
            scratch_shapes=list(scratch),
            cost_estimate=pl.CostEstimate(flops=flops, bytes_accessed=nbytes, transcendentals=0),
            compiler_params=pltpu.CompilerParams(vmem_limit_bytes=limit << 20),
        )(*args)

    return run


def images_kernel(
    info, own0, own1, right0, right1, across0, across1, left0, left1, got,
    cells, images, blocks_ref, neart_ref, fart_ref, near_ref, far_ref,
    weights, field,
):
    g = info[0]
    live = info[1]
    even = info[2] == 0
    parts = ((own0, own1), (right0, right1), (across0, across1), (left0, left1))
    rows = lax.broadcasted_iota(jnp.int32, (CX, CX), 0)
    cols = lax.broadcasted_iota(jnp.int32, (CX, CX), 1)
    gap = jnp.abs(rows - cols)
    tri = jnp.where(gap == 0, 1.0, jnp.where(gap == 1, 0.5, 0.0)).astype(F32)
    for o in range(GRP):
        for q in range(GRP):
            dist = jnp.abs(lax.rem(g + o, GRP) - lax.rem(g + q, GRP))
            coef = jnp.where(dist == 0, 1.0, jnp.where(dist == 1, 0.5, 0.0)).astype(F32)
            weights[o * CX:(o + 1) * CX, q * CX:(q + 1) * CX] = (tri * coef).astype(BF16)
    for p in range(PLANES):
        for o in range(GRP):
            plane = parts[o][p // 2][p % 2]
            cells[:, p * CELLS + o * CX:p * CELLS + (o + 1) * CX] = plane[...]
    for o in range(GRP):
        field[:, o * CX:(o + 1) * CX] = 16.0 + got[lax.rem(g + o, GRP), COLS:, :]

    def slot_half(h, carry):
        row = pl.ds(pl.multiple_of(h * HALF, HALF), HALF)
        smooth = []
        for p in range(PLANES):
            smooth.append(dot(cells[row, p * CELLS:(p + 1) * CELLS], weights[...]))
        low_plane, high_plane = smooth[0].astype(BF16), smooth[PLANES - 1].astype(BF16)
        near_ref[row, :] = jnp.where(even, high_plane, low_plane)
        far_ref[row, :] = jnp.where(even, low_plane, high_plane)
        for p in range(PLANES):
            along = smooth[p]
            if p == 0:
                along = along + 0.5 * smooth[1]
            elif p == PLANES - 1:
                along = along + 0.5 * smooth[p - 1]
            else:
                along = along + 0.5 * (smooth[p - 1] + smooth[p + 1])
            own = cells[row, p * CELLS:(p + 1) * CELLS].astype(F32)
            images[row, p * CELLS:(p + 1) * CELLS] = (
                field[p:p + 1, :] * own - 2.0 * along
            ).astype(BF16)
        for i in range(HALF // BLK):
            first_slot = pl.multiple_of(h * HALF + i * BLK, BLK)
            line = pl.ds(first_slot, BLK)
            block = dot_last(images[line, :], cells[line, :])
            pad = (gap == 0) & (first_slot + rows >= live)
            blocks_ref[:, line] = 0.5 * (block + block.T) + jnp.where(pad, 1.0, 0.0).astype(F32)
        for c in range(GRP):
            first = (PLANES - 1) * CELLS + c * CX
            low_turned = cells[row, c * CX:(c + 1) * CX].astype(F32).T.astype(BF16)
            high_turned = cells[row, first:first + CX].astype(F32).T.astype(BF16)
            neart_ref[c * CX:(c + 1) * CX, row] = jnp.where(even, high_turned, low_turned)
            fart_ref[c * CX:(c + 1) * CX, row] = jnp.where(even, low_turned, high_turned)
        return carry

    lax.fori_loop(0, SLOTS // HALF, slot_half, 0)


def matrix_kernel(info, cells, images, r_ref, d_ref, eh_ref, el_ref, t_ref):
    live = info[1]

    def slot_half(h, carry):
        row = pl.ds(pl.multiple_of(h * HALF, HALF), HALF)
        matrix = dot_last(images[row, :], cells[...])
        slot = h * HALF + lax.broadcasted_iota(jnp.int32, (HALF, SLOTS), 0)
        column = lax.broadcasted_iota(jnp.int32, (HALF, SLOTS), 1)
        matrix = matrix + jnp.where((slot == column) & (slot >= live), 1.0, 0.0).astype(F32)
        high, low = split(matrix)
        eh_ref[row, :] = high
        el_ref[row, :] = low
        return carry

    lax.fori_loop(0, SLOTS // HALF, slot_half, 0)
    local_kernel(r_ref, d_ref, eh_ref, el_ref, t_ref)


def invert2(m):
    scale = 1.0 / (m[0] * m[3] - m[1] * m[2])
    return m[3] * scale, -(m[1] * scale), -(m[2] * scale), m[0] * scale


def times2(m, n):
    return (
        m[0] * n[0] + m[1] * n[2], m[0] * n[1] + m[1] * n[3],
        m[2] * n[0] + m[3] * n[2], m[2] * n[1] + m[3] * n[3],
    )


def invert4(m):
    a = (m[0][0], m[0][1], m[1][0], m[1][1])
    b = (m[0][2], m[0][3], m[1][2], m[1][3])
    c = (m[2][0], m[2][1], m[3][0], m[3][1])
    d = (m[2][2], m[2][3], m[3][2], m[3][3])
    ai = invert2(a)
    aib, cai = times2(ai, b), times2(c, ai)
    si = invert2(tuple(u - v for u, v in zip(d, times2(c, aib))))
    x, y = times2(aib, si), times2(si, cai)
    z = tuple(u + v for u, v in zip(ai, times2(x, cai)))
    return (
        (z[0], z[1], -x[0], -x[1]), (z[2], z[3], -x[2], -x[3]),
        (-y[0], -y[1], si[0], si[1]), (-y[2], -y[3], si[2], si[3]),
    )


def inverse_kernel(blocks_ref, high_ref, low_ref, work):
    work[...] = blocks_ref[...]
    lane = lax.broadcasted_iota(jnp.int32, (8, BLK), 1)
    sub = lax.broadcasted_iota(jnp.int32, (8, BLK), 0)
    base = lane - lax.rem(lane, PANEL)
    within = lax.rem(lane, PANEL)
    group = lax.div(lax.broadcasted_iota(jnp.int32, (PANEL, BLK), 1), PANEL)
    count = PANEL // 8
    panels = BLK // PANEL
    spread = lambda t, i: jnp.broadcast_to(t[i:i + 1], (8, BLK))
    turn = lambda t, n: pltpu.roll(t, (n * PANEL) % BLK, 1) if n % panels else t
    wide = lambda m, n: jnp.dot(m, n, preferred_element_type=F32, precision=lax.Precision.HIGHEST)
    for p in range(panels):
        rows = slice(p * PANEL, (p + 1) * PANEL)
        packed = None
        for j in range(GRP):
            piece = turn(work[rows, j * BLK:(j + 1) * BLK], j - p)
            packed = piece if packed is None else jnp.where(group == j, piece, packed)
        tiles = [packed[8 * v:8 * v + 8] for v in range(count)]
        for k in range(0, PANEL, 4):
            v, q = k // 8, k % 8
            cols = [[jnp.take_along_axis(t, base + (k + c), axis=1) for t in tiles] for c in range(4)]
            pivot = invert4([[spread(cols[c][v], q + i) for c in range(4)] for i in range(4)])
            inside = (within >= k) & (within < k + 4)
            lines = [
                jnp.where(inside, jnp.where(within == k + i, 1.0, 0.0), spread(tiles[v], q + i))
                for i in range(4)
            ]
            new = [
                (pivot[i][0] * lines[0] + pivot[i][1] * lines[1])
                + (pivot[i][2] * lines[2] + pivot[i][3] * lines[3])
                for i in range(4)
            ]
            for u in range(count):
                tile = jnp.where(inside, 0.0, tiles[u]) - (
                    (cols[0][u] * new[0] + cols[1][u] * new[1])
                    + (cols[2][u] * new[2] + cols[3][u] * new[3])
                )
                if u == v:
                    for i in range(4):
                        tile = jnp.where(sub == q + i, new[i], tile)
                tiles[u] = tile
        packed = jnp.concatenate(tiles, axis=0)
        mults = []
        for j in range(GRP):
            mult = wide(turn(packed, -j)[:, :PANEL], work[rows, j * BLK:(j + 1) * BLK])
            mults.append(jnp.where(group == p, turn(packed, p - j), mult))
        for step in range(1, panels):
            other = (p + step) % panels
            others = slice(other * PANEL, (other + 1) * PANEL)
            for j in range(GRP):
                lanes = slice(j * BLK, (j + 1) * BLK)
                block = work[others, lanes]
                change = wide(turn(block, -p)[:, :PANEL], mults[j])
                work[others, lanes] = jnp.where(group == p, 0.0, block) - change
        for j in range(GRP):
            work[rows, j * BLK:(j + 1) * BLK] = mults[j]
    high, low = split(work[...])
    high_ref[...] = high
    low_ref[...] = low


def precondition(residual, ih_ref, il_ref):
    parts = []
    for j in range(GRP):
        lanes = slice(j * BLK, (j + 1) * BLK)
        high, low = split(residual[:, lanes])
        both = dot(jnp.concatenate([high, low], axis=0), ih_ref[:, lanes])
        parts.append(both[:COLS] + both[COLS:] + dot(high, il_ref[:, lanes]))
    return DAMPING * jnp.concatenate(parts, axis=1)


def send(delta, near_ref, far_ref, near_out, far_out):
    sent = delta.astype(BF16)
    far_out[...] = dot(sent, far_ref[...]).astype(BF16)
    near_out[...] = dot(sent, near_ref[...]).astype(BF16)


def first_kernel(got, ih_ref, il_ref, near_ref, far_ref, r_ref, d_ref, near_out, far_out):
    for j in range(GRP):
        r_ref[:, j * BLK:(j + 1) * BLK] = got[j, :COLS, :]
    delta = precondition(r_ref[...], ih_ref, il_ref)
    d_ref[...] = delta
    send(delta, near_ref, far_ref, near_out, far_out)


def local_kernel(r_ref, d_ref, eh_ref, el_ref, t_ref):
    high, low = split(d_ref[...])
    both = dot(jnp.concatenate([high, low], axis=0), eh_ref[...])
    t_ref[...] = r_ref[...] - (both[:COLS] + both[COLS:] + dot(high, el_ref[...]))


def sweep_kernel(
    t_ref, far_in, near_in, neart_ref, fart_ref, ih_ref, il_ref, near_ref, far_ref,
    r_ref, d_ref, near_out, far_out,
):
    residual = t_ref[...] + dot(near_in[...], neart_ref[...]) + dot(far_in[...], fart_ref[...])
    r_ref[...] = residual
    delta = precondition(residual, ih_ref, il_ref)
    d_ref[...] = delta
    send(delta, near_ref, far_ref, near_out, far_out)


def both_kernel(r_ref, d_ref, x_ref, eh_ref, el_ref, t_ref, new_ref):
    new_ref[...] = x_ref[...] + d_ref[...]
    local_kernel(r_ref, d_ref, eh_ref, el_ref, t_ref)


def last_kernel(t_ref, x_ref, far_in, near_in, neart_ref, fart_ref, ih_ref, il_ref, out_ref):
    residual = t_ref[...] + dot(near_in[...], neart_ref[...]) + dot(far_in[...], fart_ref[...])
    out_ref[...] = x_ref[...] + precondition(residual, ih_ref, il_ref)


def shift_by(values, offset):
    return lax.ppermute(values, "grp", [(i, (i + offset) % GRP) for i in range(GRP)])


def on_device_steps(deflation, shift_field, counts, right_sides):
    g = lax.axis_index("grp")
    subs = lax.axis_size("sub")
    live_count = counts[0]
    parity = lax.rem(lax.axis_index("sub"), 2)
    info = jnp.stack([g.astype(jnp.int32), live_count, parity.astype(jnp.int32)])
    slot_ids = lax.iota(jnp.int32, SLOTS)
    live = slot_ids < live_count
    masked = jnp.where(live[:, None, None, None], deflation, jnp.zeros((), BF16))
    planes = jnp.transpose(masked.reshape(SLOTS, PLANES, CX), (1, 0, 2))
    own0, own1 = planes[:2], planes[2:]
    row_slot = g * BLK + lax.iota(jnp.int32, BLK)
    rhs = jnp.where((row_slot >= live_count)[:, None], 0.0, right_sides).T.reshape(GRP, COLS, BLK)
    field = jnp.zeros((8, CX), F32).at[:PLANES].set(shift_field.reshape(PLANES, CX))
    pieces = jnp.concatenate([rhs, jnp.broadcast_to(field, (GRP, 8, CX))], axis=1)
    left0 = shift_by(own0, 1)
    right1 = shift_by(own1, -1)
    left1 = shift_by(own1, 1)
    right0 = shift_by(own0, -1)
    across0 = shift_by(left0, 1)
    across1 = shift_by(right1, -1)
    got = lax.all_to_all(pieces, "grp", 0, 0)

    square = (SLOTS, SLOTS)
    tall = (SLOTS, PLANES * CELLS)
    cells, images, blocks, neart, fart, near, far = call(
        images_kernel,
        [(tall, BF16), (tall, BF16), ((BLK, SLOTS), F32)] + [(square, BF16)] * 4,
        scratch=[pltpu.VMEM((CELLS, CELLS), BF16), pltpu.VMEM((8, CELLS), F32)],
        limit=24,
        flops=2 * 10**9,
        nbytes=8 << 20,
    )(info, own0, own1, right0, right1, across0, across1, left0, left1, got)
    ih, il = call(
        inverse_kernel,
        [((BLK, SLOTS), BF16)] * 2,
        scratch=[pltpu.VMEM((BLK, SLOTS), F32)],
        flops=10**9,
        nbytes=1 << 19,
    )(blocks)

    vec = (COLS, SLOTS)
    r, d, near_msg, far_msg = call(
        first_kernel, [(vec, F32), (vec, F32), (vec, BF16), (vec, BF16)],
        flops=10**8, nbytes=1 << 20,
    )(got, ih, il, near, far)
    x = d
    near_pairs = [(i, i ^ 1) for i in range(subs)]
    far_pairs = [(i, ((i + 1) ^ 1) - 1) for i in range(1, subs - 1)]
    for sweep in range(1, SWEEPS):
        far_got = lax.ppermute(far_msg, "sub", far_pairs)
        near_got = lax.ppermute(near_msg, "sub", near_pairs)
        if sweep == 1:
            eh, el, t = call(
                matrix_kernel, [(square, BF16), (square, BF16), (vec, F32)],
                limit=16, flops=10**9, nbytes=5 << 20,
            )(info, cells, images, r, d)
        else:
            t, x = call(
                both_kernel, [(vec, F32), (vec, F32)], flops=10**8, nbytes=1 << 20,
            )(r, d, x, eh, el)
        if sweep < SWEEPS - 1:
            r, d, near_msg, far_msg = call(
                sweep_kernel, [(vec, F32), (vec, F32), (vec, BF16), (vec, BF16)],
                flops=2 * 10**8, nbytes=3 << 20,
            )(t, far_got, near_got, neart, fart, ih, il, near, far)
        else:
            (x,) = call(
                last_kernel, [(vec, F32)], flops=10**8, nbytes=2 << 20,
            )(t, x, far_got, near_got, neart, fart, ih, il)
    return lax.all_to_all(x, "grp", 1, 0, tiled=True).T


def solution(mesh):
    in_specs = (
        P(None, "sub", "grp", None),
        P("sub", "grp", None),
        P("sub"),
        P(("sub", "grp"), None),
    )
    return jax.shard_map(
        on_device_steps, mesh=mesh, in_specs=in_specs,
        out_specs=P(("sub", "grp"), None), check_vma=False,
    )
```

time: 110 us -> 105 us (0.955)
  starting transfers between devices: 58 us -> 63.2 us
  waiting for transfers between devices: 15 us -> 10.3 us
  Pallas kernels: 21.1 us -> 18.3 us
  blocking collectives: 10.7 us -> 8.36 us
    ppermute x4 -> x6, waiting for transfers between devices: 10.4 us -> 0.02 us  [shift_by(): lax.ppermute(values, 'grp', [(i, (i + offset) % GRP) for i in range(GRP)])]
    all_to_all x1, waiting for transfers between devices: 0.01 us -> 5.99 us  [on_device_steps(): got = lax.all_to_all(pieces, 'grp', 0, 0)]
    ppermute x4 -> x6, starting transfers between devices: 14.1 us -> 19.5 us  [shift_by(): lax.ppermute(values, 'grp', [(i, (i + offset) % GRP) for i in range(GRP)])]
    pallas_call x13, Pallas kernels: 21.1 us -> 18.3 us  [run(): pl.pallas_call(kernel, out_shape=[jax.ShapeDtypeStruct(s, d) for s, d in...]
    all_to_all x1, blocking collectives: 10.7 us -> 8.36 us  [on_device_steps(): return lax.all_to_all(x, 'grp', 1, 0, tiled=True).T]
    ppermute x10, starting transfers between devices: 40.5 us -> 39.3 us  [the longest x5 29.7 us: on_device_steps(): far_got = lax.ppermute(far_msg, 'sub', far_pairs)]
    all_to_all x1, starting transfers between devices: 3.33 us -> 4.49 us  [on_device_steps(): got = lax.all_to_all(pieces, 'grp', 0, 0)]
  transfers between devices with their start and end apart: 15 -> 17, of which waited for: 8 -> 5; matrix products, arithmetic and copies ran while one was open for 1% -> 1% of each run, Pallas kernels for 1% -> 3%
where the time goes in v2:
time: 105 us; the launch traced here: 104 us
  starting transfers between devices  63.2 us (60%)
  Pallas kernels  18.3 us (17%)
  waiting for transfers between devices  10.3 us (10%)
  blocking collectives  8.36 us (8%)
  other arithmetic  2.03 us (2%)
    ppermute x5, starting transfers between devices, on_device_steps(): far_got = lax.ppermute(far_msg, 'sub', far_pairs)  29.7 us
    ppermute x6, starting transfers between devices, shift_by(): lax.ppermute(values, 'grp', [(i, (i + offset) % GRP) for i in range(GRP)])  19.5 us
    pallas_call x13, Pallas kernels, run(): pl.pallas_call(kernel, out_shape=[jax.ShapeDtypeStruct(s, d) for s, d in...  18.3 us
    ppermute x5, starting transfers between devices, on_device_steps(): near_got = lax.ppermute(near_msg, 'sub', near_pairs)  9.6 us
    all_to_all x1, blocking collectives, on_device_steps(): return lax.all_to_all(x, 'grp', 1, 0, tiled=True).T  8.36 us
    all_to_all x1, waiting for transfers between devices, on_device_steps(): got = lax.all_to_all(pieces, 'grp', 0, 0)  5.99 us
    all_to_all x1, starting transfers between devices, on_device_steps(): got = lax.all_to_all(pieces, 'grp', 0, 0)  4.49 us
    ppermute x5, waiting for transfers between devices, on_device_steps(): far_got = lax.ppermute(far_msg, 'sub', far_pairs)  4.26 us
  transfers between devices with their start and end apart: 17, of which 5 were waited for; matrix products, arithmetic and copies ran while one was open for 1% of the time, Pallas kernels for 3%

profile of v2, /device:TPU:32, one launch (start us, length us, event | category | flops | bytes accessed | tf_op | source)
XLA Modules:
  0.0 104.1 jit_solution(16171579025628800909)
XLA Ops:
  0.0 0.0 copy-start
  0.0 0.0 copy-start.1
  0.7 1.2 %fusion = bf16[4,512,128]{2,1,0:T(8,128)(2,1)S(1)} fusion(bf16[512,4,1,128]{3,1,2,0:T(4,128)(2,1)} %param.6, pred[512]{0:T(512)(128)(4,1)S(1)} %iota_compare_fusion), kind=kLoop, calls=%fused_computation.1 | loop fusion | flops 262144 | bytes 1049088 | tf_op jit(solution)/shard_map/transpose | solution.py:289
  1.9 4.7 %collective-permute-start.1 = (bf16[2,512,128]{2,1,0:T(8,128)(2,1)S(1)}, bf16[2,512,128]{2,1,0:T(8,128)(2,1)S(1)}, u32[]{:S(2)}, u32[]{:S(2)}) collective-permute-start(bf16[2,512,128]{2,1,0:T(8,128)(2,1)S(1)} %get-tuple-element.97.own1), channel_id=1, source_target_pairs={{0,3},{1,0},{2,1},{3,2},{4,7},{5,4},{6,5},{7,6},{8,11},{9,8},{10,9... | collective-permute-start | bytes 786440 | tf_op jit(solution)/shard_map/ppermute | solution.py:277
  6.6 1.9 %collective-permute-start.2 = (bf16[2,512,128]{2,1,0:T(8,128)(2,1)S(1)}, bf16[2,512,128]{2,1,0:T(8,128)(2,1)S(1)}, u32[]{:S(2)}, u32[]{:S(2)}) collective-permute-start(bf16[2,512,128]{2,1,0:T(8,128)(2,1)S(1)} %get-tuple-element.98.own0), channel_id=1, source_target_pairs={{0,1},{1,2},{2,3},{3,0},{4,5},{5,6},{6,7},{7,4},{8,9},{9,10},{10,1... | collective-permute-start | bytes 786440 | tf_op jit(solution)/shard_map/ppermute | solution.py:277
  8.5 2.7 %collective-permute-start.5 = (bf16[2,512,128]{2,1,0:T(8,128)(2,1)S(1)}, bf16[2,512,128]{2,1,0:T(8,128)(2,1)S(1)}, u32[]{:S(2)}, u32[]{:S(2)}) collective-permute-start(bf16[2,512,128]{2,1,0:T(8,128)(2,1)S(1)} %get-tuple-element.97.own1), channel_id=1, source_target_pairs={{0,1},{1,2},{2,3},{3,0},{4,5},{5,6},{6,7},{7,4},{8,9},{9,10},{10,1... | collective-permute-start | bytes 786440 | tf_op jit(solution)/shard_map/ppermute | solution.py:277
  11.2 4.4 %collective-permute-start = (bf16[2,512,128]{2,1,0:T(8,128)(2,1)S(1)}, bf16[2,512,128]{2,1,0:T(8,128)(2,1)S(1)}, u32[]{:S(2)}, u32[]{:S(2)}) collective-permute-start(bf16[2,512,128]{2,1,0:T(8,128)(2,1)S(1)} %get-tuple-element.98.own0), channel_id=1, source_target_pairs={{0,3},{1,0},{2,1},{3,2},{4,7},{5,4},{6,5},{7,6},{8,11},{9,8},{10,9... | collective-permute-start | bytes 786440 | tf_op jit(solution)/shard_map/ppermute | solution.py:277
  15.6 0.0 collective-permute-done.1.right1
  15.6 3.9 %collective-permute-start.4 = (bf16[2,512,128]{2,1,0:T(8,128)(2,1)S(1)}, bf16[2,512,128]{2,1,0:T(8,128)(2,1)S(1)}, u32[]{:S(2)}, u32[]{:S(2)}) collective-permute-start(bf16[2,512,128]{2,1,0:T(8,128)(2,1)S(1)} %collective-permute-done.1.right1), channel_id=1, source_target_pairs={{0,3},{1,0},{2,1},{3,2},{4,7},{5,4},{6,5},{7,6},{8,11},{9,8},{10,9... | collective-permute-start | bytes 786440 | tf_op jit(solution)/shard_map/ppermute | solution.py:277
  19.6 0.0 collective-permute-done.2.left0
  19.6 1.9 %collective-permute-start.3 = (bf16[2,512,128]{2,1,0:T(8,128)(2,1)S(1)}, bf16[2,512,128]{2,1,0:T(8,128)(2,1)S(1)}, u32[]{:S(2)}, u32[]{:S(2)}) collective-permute-start(bf16[2,512,128]{2,1,0:T(8,128)(2,1)S(1)} %collective-permute-done.2.left0), channel_id=1, source_target_pairs={{0,1},{1,2},{2,3},{3,0},{4,5},{5,6},{6,7},{7,4},{8,9},{9,10},{10,1... | collective-permute-start | bytes 786440 | tf_op jit(solution)/shard_map/ppermute | solution.py:277
  21.5 0.0 copy-done
  21.5 0.1 select_bitcast_fusion
  21.6 0.1 copy.9
  21.7 0.0 copy-done.1
  21.7 0.7 pad_maximum_fusion
  22.4 4.5 %all-to-all-start = ((f32[4,72,128]{2,1,0:T(8,128)}), f32[4,72,128]{2,1,0:T(8,128)S(1)}, u32[]{:S(2)}, u32[]{:S(2)}) async-start(f32[4,72,128]{2,1,0:T(8,128)} %pad_maximum_fusion), calls=%async_computation | async-start | bytes 294912 | tf_op jit(solution)/shard_map/all_to_all | solution.py:301
  26.9 0.1 pad_add_fusion.info
  27.0 6.0 %all-to-all-done.got = f32[4,72,128]{2,1,0:T(8,128)S(1)} async-done(((f32[4,72,128]{2,1,0:T(8,128)}), f32[4,72,128]{2,1,0:T(8,128)S(1)}, u32[]{:S(2)}, u32[]{:S(2)}) %all-to-all-start) | async-done | bytes 147488 | tf_op jit(solution)/shard_map/all_to_all | solution.py:301
  33.0 0.0 collective-permute-done.5.left1
  33.0 0.0 collective-permute-done.right0
  33.0 0.0 collective-permute-done.4.across1
  33.0 0.0 collective-permute-done.3.across0
  33.0 4.4 %shard_map.46 = (bf16[512,2048]{1,0:T(8,128)(2,1)S(1)}, bf16[512,2048]{1,0:T(8,128)(2,1)S(1)}, f32[128,512]{1,0:T(8,128)S(1)}, bf16[512,512]{1,0:T(8,128)(2,1)S(...) custom-call(s32[3]{0:T(128)S(1)} %pad_add_fusion.info, ...), custom_call_target="tpu_custom_call" | custom-call | flops 2000000000 | bytes 8388608 | tf_op jit(solution)/shard_map/pallas_call | solution.py:42
  37.4 6.6 %shard_map.47 = (bf16[128,512]{1,0:T(8,128)(2,1)S(1)}, bf16[128,512]{1,0:T(8,128)(2,1)S(1)}) custom-call(f32[128,512]{1,0:T(8,128)S(1)} %get-tuple-element.59.blocks_ref), custom_call_target="tpu_custom_call" | custom-call | flops 1000000000 | bytes 524288 | tf_op jit(solution)/shard_map/pallas_call | solution.py:42
  44.0 0.4 shard_map.48
  44.4 7.3 %collective-permute-start.6 = (bf16[64,512]{1,0:T(8,128)(2,1)S(1)}, bf16[64,512]{1,0:T(8,128)(2,1)S(1)}, u32[]{:S(2)}, u32[]{:S(2)}) collective-permute-start(bf16[64,512]{1,0:T(8,128)(2,1)S(1)} %get-tuple-element.67), channel_id=1, source_target_pairs={{4,8},{8,4},{12,16},{16,12},{20,24},{24,20},{28,32},{32,28},{36,40... | collective-permute-start | bytes 196616 | tf_op jit(solution)/shard_map/ppermute | solution.py:330
  51.7 1.9 %collective-permute-start.7 = (bf16[64,512]{1,0:T(8,128)(2,1)S(1)}, bf16[64,512]{1,0:T(8,128)(2,1)S(1)}, u32[]{:S(2)}, u32[]{:S(2)}) collective-permute-start(bf16[64,512]{1,0:T(8,128)(2,1)S(1)} %get-tuple-element.68), channel_id=1, source_target_pairs={{0,4},{4,0},{8,12},{12,8},{16,20},{20,16},{24,28},{28,24},{32,36},... | collective-permute-start | bytes 196616 | tf_op jit(solution)/shard_map/ppermute | solution.py:331
  53.6 2.4 %shard_map.49 = (bf16[512,512]{1,0:T(8,128)(2,1)S(1)}, bf16[512,512]{1,0:T(8,128)(2,1)S(1)}, f32[64,512]{1,0:T(8,128)S(1)}) custom-call(s32[3]{0:T(128)S(1)} %pad_add_fusion.info, bf16[512,2048]{1,0:T(8,128)(2,1)S(1)} %get-tuple-element.57.cells, bf16[512,2048]{1,0:T(8,128)(2,1)S(1)} %get-tuple-element.58.images, f32[64,512]{1,0:T(8,128)S(1)} %get-tuple-element.64.r_ref, ...), custom_call_target="tpu_custom_call" | custom-call | flops 1000000000 | bytes 5242880 | tf_op jit(solution)/shard_map/pallas_call | solution.py:42
  56.0 0.0 collective-permute-done.6.far_in
  56.0 0.0 collective-permute-done.7.near_in
  56.0 0.7 shard_map.50
  56.7 5.6 %collective-permute-start.8 = (bf16[64,512]{1,0:T(8,128)(2,1)S(1)}, bf16[64,512]{1,0:T(8,128)(2,1)S(1)}, u32[]{:S(2)}, u32[]{:S(2)}) collective-permute-start(bf16[64,512]{1,0:T(8,128)(2,1)S(1)} %get-tuple-element.76), channel_id=1, source_target_pairs={{4,8},{8,4},{12,16},{16,12},{20,24},{24,20},{28,32},{32,28},{36,40... | collective-permute-start | bytes 196616 | tf_op jit(solution)/shard_map/ppermute | solution.py:330
  62.4 1.9 %collective-permute-start.9 = (bf16[64,512]{1,0:T(8,128)(2,1)S(1)}, bf16[64,512]{1,0:T(8,128)(2,1)S(1)}, u32[]{:S(2)}, u32[]{:S(2)}) collective-permute-start(bf16[64,512]{1,0:T(8,128)(2,1)S(1)} %get-tuple-element.77), channel_id=1, source_target_pairs={{0,4},{4,0},{8,12},{12,8},{16,20},{20,16},{24,28},{28,24},{32,36},... | collective-permute-start | bytes 196616 | tf_op jit(solution)/shard_map/ppermute | solution.py:331
  64.3 0.3 shard_map.51
  64.6 1.1 %collective-permute-done.8.far_in = bf16[64,512]{1,0:T(8,128)(2,1)S(1)} collective-permute-done((bf16[64,512]{1,0:T(8,128)(2,1)S(1)}, bf16[64,512]{1,0:T(8,128)(2,1)S(1)}, u32[]{:S(2)}, u32[]{:S(2)}) %collective-permute-start.8) | collective-permute-done | bytes 65568 | tf_op jit(solution)/shard_map/ppermute | solution.py:330
  65.7 0.0 collective-permute-done.9.near_in
  65.7 0.7 shard_map.52
  66.4 5.6 %collective-permute-start.10 = (bf16[64,512]{1,0:T(8,128)(2,1)S(1)}, bf16[64,512]{1,0:T(8,128)(2,1)S(1)}, u32[]{:S(2)}, u32[]{:S(2)}) collective-permute-start(bf16[64,512]{1,0:T(8,128)(2,1)S(1)} %get-tuple-element.82), channel_id=1, source_target_pairs={{4,8},{8,4},{12,16},{16,12},{20,24},{24,20},{28,32},{32,28},{36,40... | collective-permute-start | bytes 196616 | tf_op jit(solution)/shard_map/ppermute | solution.py:330
  72.0 1.9 %collective-permute-start.11 = (bf16[64,512]{1,0:T(8,128)(2,1)S(1)}, bf16[64,512]{1,0:T(8,128)(2,1)S(1)}, u32[]{:S(2)}, u32[]{:S(2)}) collective-permute-start(bf16[64,512]{1,0:T(8,128)(2,1)S(1)} %get-tuple-element.83), channel_id=1, source_target_pairs={{0,4},{4,0},{8,12},{12,8},{16,20},{20,16},{24,28},{28,24},{32,36},... | collective-permute-start | bytes 196616 | tf_op jit(solution)/shard_map/ppermute | solution.py:331
  73.9 0.3 shard_map.53
  74.2 1.1 %collective-permute-done.10.far_in = bf16[64,512]{1,0:T(8,128)(2,1)S(1)} collective-permute-done((bf16[64,512]{1,0:T(8,128)(2,1)S(1)}, bf16[64,512]{1,0:T(8,128)(2,1)S(1)}, u32[]{:S(2)}, u32[]{:S(2)}) %collective-permute-start.10) | collective-permute-done | bytes 65568 | tf_op jit(solution)/shard_map/ppermute | solution.py:330
  75.3 0.0 collective-permute-done.11.near_in
  75.3 0.7 shard_map.54
  76.0 5.6 %collective-permute-start.12 = (bf16[64,512]{1,0:T(8,128)(2,1)S(1)}, bf16[64,512]{1,0:T(8,128)(2,1)S(1)}, u32[]{:S(2)}, u32[]{:S(2)}) collective-permute-start(bf16[64,512]{1,0:T(8,128)(2,1)S(1)} %get-tuple-element.88), channel_id=1, source_target_pairs={{4,8},{8,4},{12,16},{16,12},{20,24},{24,20},{28,32},{32,28},{36,40... | collective-permute-start | bytes 196616 | tf_op jit(solution)/shard_map/ppermute | solution.py:330
  81.6 1.9 %collective-permute-start.13 = (bf16[64,512]{1,0:T(8,128)(2,1)S(1)}, bf16[64,512]{1,0:T(8,128)(2,1)S(1)}, u32[]{:S(2)}, u32[]{:S(2)}) collective-permute-start(bf16[64,512]{1,0:T(8,128)(2,1)S(1)} %get-tuple-element.89), channel_id=1, source_target_pairs={{0,4},{4,0},{8,12},{12,8},{16,20},{20,16},{24,28},{28,24},{32,36},... | collective-permute-start | bytes 196616 | tf_op jit(solution)/shard_map/ppermute | solution.py:331
  83.5 0.3 shard_map.55
  83.8 1.1 %collective-permute-done.12.far_in = bf16[64,512]{1,0:T(8,128)(2,1)S(1)} collective-permute-done((bf16[64,512]{1,0:T(8,128)(2,1)S(1)}, bf16[64,512]{1,0:T(8,128)(2,1)S(1)}, u32[]{:S(2)}, u32[]{:S(2)}) %collective-permute-start.12) | collective-permute-done | bytes 65568 | tf_op jit(solution)/shard_map/ppermute | solution.py:330
  84.9 0.0 collective-permute-done.13.near_in
  84.9 0.7 shard_map.56
  85.6 5.6 %collective-permute-start.14 = (bf16[64,512]{1,0:T(8,128)(2,1)S(1)}, bf16[64,512]{1,0:T(8,128)(2,1)S(1)}, u32[]{:S(2)}, u32[]{:S(2)}) collective-permute-start(bf16[64,512]{1,0:T(8,128)(2,1)S(1)} %get-tuple-element.95), channel_id=1, source_target_pairs={{4,8},{8,4},{12,16},{16,12},{20,24},{24,20},{28,32},{32,28},{36,40... | collective-permute-start | bytes 196616 | tf_op jit(solution)/shard_map/ppermute | solution.py:330
  91.2 1.9 %collective-permute-start.15 = (bf16[64,512]{1,0:T(8,128)(2,1)S(1)}, bf16[64,512]{1,0:T(8,128)(2,1)S(1)}, u32[]{:S(2)}, u32[]{:S(2)}) collective-permute-start(bf16[64,512]{1,0:T(8,128)(2,1)S(1)} %get-tuple-element.96), channel_id=1, source_target_pairs={{0,4},{4,0},{8,12},{12,8},{16,20},{20,16},{24,28},{28,24},{32,36},... | collective-permute-start | bytes 196616 | tf_op jit(solution)/shard_map/ppermute | solution.py:331
  93.1 0.3 shard_map.57
  93.5 1.1 %collective-permute-done.14.far_in = bf16[64,512]{1,0:T(8,128)(2,1)S(1)} collective-permute-done((bf16[64,512]{1,0:T(8,128)(2,1)S(1)}, bf16[64,512]{1,0:T(8,128)(2,1)S(1)}, u32[]{:S(2)}, u32[]{:S(2)}) %collective-permute-start.14) | collective-permute-done | bytes 65568 | tf_op jit(solution)/shard_map/ppermute | solution.py:330
  94.5 0.0 collective-permute-done.15.near_in
  94.5 0.5 shard_map.58
  95.0 8.4 %all_to_all.24 = f32[64,4,128]{2,0,1:T(8,128)S(1)} all-to-all(f32[64,4,128]{2,0,1:T(8,128)S(1)} %copy_bitcast_fusion), channel_id=1, replica_groups=mesh['sub'=128,'grp'=4] {'grp'}, dimensions={1} | all-to-all | bytes 262144 | tf_op jit(solution)/shard_map/all_to_all | solution.py:350
  103.4 0.8 copy.11
  (6 shorter events, 0.1 us)
Async XLA Ops:
  0.0 21.5 %copy-start = (f32[128,256]{1,0:T(8,128)S(1)}, f32[128,256]{1,0:T(8,128)}, u32[]{:S(2)}) copy-start(f32[128,256]{1,0:T(8,128)} %param.9) | copy-start | bytes 393220
  0.0 21.7 %copy-start.1 = (f32[4,1,128]{2,1,0:T(1,128)S(1)}, f32[4,1,128]{2,1,0:T(1,128)}, u32[]{:S(2)}) copy-start(f32[4,1,128]{2,1,0:T(1,128)} %param.7) | copy-start | bytes 6148
  1.9 13.7 %collective-permute-start.1 = (bf16[2,512,128]{2,1,0:T(8,128)(2,1)S(1)}, bf16[2,512,128]{2,1,0:T(8,128)(2,1)S(1)}, u32[]{:S(2)}, u32[]{:S(2)}) collective-permute-start(bf16[2,512,128]{2,1,0:T(8,128)(2,1)S(1)} %get-tuple-element.97.own1), channel_id=1, source_target_pairs={{0,3},{1,0},{2,1},{3,2},{4,7},{5,4},{6,5},{7,6},{8,11},{9,8},{10,9... | collective-permute-start | bytes 786440 | tf_op jit(solution)/shard_map/ppermute | solution.py:277
  6.6 13.0 %collective-permute-start.2 = (bf16[2,512,128]{2,1,0:T(8,128)(2,1)S(1)}, bf16[2,512,128]{2,1,0:T(8,128)(2,1)S(1)}, u32[]{:S(2)}, u32[]{:S(2)}) collective-permute-start(bf16[2,512,128]{2,1,0:T(8,128)(2,1)S(1)} %get-tuple-element.98.own0), channel_id=1, source_target_pairs={{0,1},{1,2},{2,3},{3,0},{4,5},{5,6},{6,7},{7,4},{8,9},{9,10},{10,1... | collective-permute-start | bytes 786440 | tf_op jit(solution)/shard_map/ppermute | solution.py:277
  8.5 24.4 %collective-permute-start.5 = (bf16[2,512,128]{2,1,0:T(8,128)(2,1)S(1)}, bf16[2,512,128]{2,1,0:T(8,128)(2,1)S(1)}, u32[]{:S(2)}, u32[]{:S(2)}) collective-permute-start(bf16[2,512,128]{2,1,0:T(8,128)(2,1)S(1)} %get-tuple-element.97.own1), channel_id=1, source_target_pairs={{0,1},{1,2},{2,3},{3,0},{4,5},{5,6},{6,7},{7,4},{8,9},{9,10},{10,1... | collective-permute-start | bytes 786440 | tf_op jit(solution)/shard_map/ppermute | solution.py:277
  11.2 21.8 %collective-permute-start = (bf16[2,512,128]{2,1,0:T(8,128)(2,1)S(1)}, bf16[2,512,128]{2,1,0:T(8,128)(2,1)S(1)}, u32[]{:S(2)}, u32[]{:S(2)}) collective-permute-start(bf16[2,512,128]{2,1,0:T(8,128)(2,1)S(1)} %get-tuple-element.98.own0), channel_id=1, source_target_pairs={{0,3},{1,0},{2,1},{3,2},{4,7},{5,4},{6,5},{7,6},{8,11},{9,8},{10,9... | collective-permute-start | bytes 786440 | tf_op jit(solution)/shard_map/ppermute | solution.py:277
  15.6 17.3 %collective-permute-start.4 = (bf16[2,512,128]{2,1,0:T(8,128)(2,1)S(1)}, bf16[2,512,128]{2,1,0:T(8,128)(2,1)S(1)}, u32[]{:S(2)}, u32[]{:S(2)}) collective-permute-start(bf16[2,512,128]{2,1,0:T(8,128)(2,1)S(1)} %collective-permute-done.1.right1), channel_id=1, source_target_pairs={{0,3},{1,0},{2,1},{3,2},{4,7},{5,4},{6,5},{7,6},{8,11},{9,8},{10,9... | collective-permute-start | bytes 786440 | tf_op jit(solution)/shard_map/ppermute | solution.py:277
  19.6 13.4 %collective-permute-start.3 = (bf16[2,512,128]{2,1,0:T(8,128)(2,1)S(1)}, bf16[2,512,128]{2,1,0:T(8,128)(2,1)S(1)}, u32[]{:S(2)}, u32[]{:S(2)}) collective-permute-start(bf16[2,512,128]{2,1,0:T(8,128)(2,1)S(1)} %collective-permute-done.2.left0), channel_id=1, source_target_pairs={{0,1},{1,2},{2,3},{3,0},{4,5},{5,6},{6,7},{7,4},{8,9},{9,10},{10,1... | collective-permute-start | bytes 786440 | tf_op jit(solution)/shard_map/ppermute | solution.py:277
  22.4 10.6 %all-to-all-start = ((f32[4,72,128]{2,1,0:T(8,128)}), f32[4,72,128]{2,1,0:T(8,128)S(1)}, u32[]{:S(2)}, u32[]{:S(2)}) async-start(f32[4,72,128]{2,1,0:T(8,128)} %pad_maximum_fusion), calls=%async_computation | async-start | bytes 294912 | tf_op jit(solution)/shard_map/all_to_all | solution.py:301
  44.4 11.6 %collective-permute-start.6 = (bf16[64,512]{1,0:T(8,128)(2,1)S(1)}, bf16[64,512]{1,0:T(8,128)(2,1)S(1)}, u32[]{:S(2)}, u32[]{:S(2)}) collective-permute-start(bf16[64,512]{1,0:T(8,128)(2,1)S(1)} %get-tuple-element.67), channel_id=1, source_target_pairs={{4,8},{8,4},{12,16},{16,12},{20,24},{24,20},{28,32},{32,28},{36,40... | collective-permute-start | bytes 196616 | tf_op jit(solution)/shard_map/ppermute | solution.py:330
  51.7 4.3 %collective-permute-start.7 = (bf16[64,512]{1,0:T(8,128)(2,1)S(1)}, bf16[64,512]{1,0:T(8,128)(2,1)S(1)}, u32[]{:S(2)}, u32[]{:S(2)}) collective-permute-start(bf16[64,512]{1,0:T(8,128)(2,1)S(1)} %get-tuple-element.68), channel_id=1, source_target_pairs={{0,4},{4,0},{8,12},{12,8},{16,20},{20,16},{24,28},{28,24},{32,36},... | collective-permute-start | bytes 196616 | tf_op jit(solution)/shard_map/ppermute | solution.py:331
  56.7 8.9 %collective-permute-start.8 = (bf16[64,512]{1,0:T(8,128)(2,1)S(1)}, bf16[64,512]{1,0:T(8,128)(2,1)S(1)}, u32[]{:S(2)}, u32[]{:S(2)}) collective-permute-start(bf16[64,512]{1,0:T(8,128)(2,1)S(1)} %get-tuple-element.76), channel_id=1, source_target_pairs={{4,8},{8,4},{12,16},{16,12},{20,24},{24,20},{28,32},{32,28},{36,40... | collective-permute-start | bytes 196616 | tf_op jit(solution)/shard_map/ppermute | solution.py:330
  62.4 3.3 %collective-permute-start.9 = (bf16[64,512]{1,0:T(8,128)(2,1)S(1)}, bf16[64,512]{1,0:T(8,128)(2,1)S(1)}, u32[]{:S(2)}, u32[]{:S(2)}) collective-permute-start(bf16[64,512]{1,0:T(8,128)(2,1)S(1)} %get-tuple-element.77), channel_id=1, source_target_pairs={{0,4},{4,0},{8,12},{12,8},{16,20},{20,16},{24,28},{28,24},{32,36},... | collective-permute-start | bytes 196616 | tf_op jit(solution)/shard_map/ppermute | solution.py:331
  66.4 8.9 %collective-permute-start.10 = (bf16[64,512]{1,0:T(8,128)(2,1)S(1)}, bf16[64,512]{1,0:T(8,128)(2,1)S(1)}, u32[]{:S(2)}, u32[]{:S(2)}) collective-permute-start(bf16[64,512]{1,0:T(8,128)(2,1)S(1)} %get-tuple-element.82), channel_id=1, source_target_pairs={{4,8},{8,4},{12,16},{16,12},{20,24},{24,20},{28,32},{32,28},{36,40... | collective-permute-start | bytes 196616 | tf_op jit(solution)/shard_map/ppermute | solution.py:330
  72.0 3.3 %collective-permute-start.11 = (bf16[64,512]{1,0:T(8,128)(2,1)S(1)}, bf16[64,512]{1,0:T(8,128)(2,1)S(1)}, u32[]{:S(2)}, u32[]{:S(2)}) collective-permute-start(bf16[64,512]{1,0:T(8,128)(2,1)S(1)} %get-tuple-element.83), channel_id=1, source_target_pairs={{0,4},{4,0},{8,12},{12,8},{16,20},{20,16},{24,28},{28,24},{32,36},... | collective-permute-start | bytes 196616 | tf_op jit(solution)/shard_map/ppermute | solution.py:331
  76.0 8.9 %collective-permute-start.12 = (bf16[64,512]{1,0:T(8,128)(2,1)S(1)}, bf16[64,512]{1,0:T(8,128)(2,1)S(1)}, u32[]{:S(2)}, u32[]{:S(2)}) collective-permute-start(bf16[64,512]{1,0:T(8,128)(2,1)S(1)} %get-tuple-element.88), channel_id=1, source_target_pairs={{4,8},{8,4},{12,16},{16,12},{20,24},{24,20},{28,32},{32,28},{36,40... | collective-permute-start | bytes 196616 | tf_op jit(solution)/shard_map/ppermute | solution.py:330
  81.6 3.3 %collective-permute-start.13 = (bf16[64,512]{1,0:T(8,128)(2,1)S(1)}, bf16[64,512]{1,0:T(8,128)(2,1)S(1)}, u32[]{:S(2)}, u32[]{:S(2)}) collective-permute-start(bf16[64,512]{1,0:T(8,128)(2,1)S(1)} %get-tuple-element.89), channel_id=1, source_target_pairs={{0,4},{4,0},{8,12},{12,8},{16,20},{20,16},{24,28},{28,24},{32,36},... | collective-permute-start | bytes 196616 | tf_op jit(solution)/shard_map/ppermute | solution.py:331
  85.6 8.9 %collective-permute-start.14 = (bf16[64,512]{1,0:T(8,128)(2,1)S(1)}, bf16[64,512]{1,0:T(8,128)(2,1)S(1)}, u32[]{:S(2)}, u32[]{:S(2)}) collective-permute-start(bf16[64,512]{1,0:T(8,128)(2,1)S(1)} %get-tuple-element.95), channel_id=1, source_target_pairs={{4,8},{8,4},{12,16},{16,12},{20,24},{24,20},{28,32},{32,28},{36,40... | collective-permute-start | bytes 196616 | tf_op jit(solution)/shard_map/ppermute | solution.py:330
  91.2 3.3 %collective-permute-start.15 = (bf16[64,512]{1,0:T(8,128)(2,1)S(1)}, bf16[64,512]{1,0:T(8,128)(2,1)S(1)}, u32[]{:S(2)}, u32[]{:S(2)}) collective-permute-start(bf16[64,512]{1,0:T(8,128)(2,1)S(1)} %get-tuple-element.96), channel_id=1, source_target_pairs={{0,4},{4,0},{8,12},{12,8},{16,20},{20,16},{24,28},{28,24},{32,36},... | collective-permute-start | bytes 196616 | tf_op jit(solution)/shard_map/ppermute | solution.py:331

commit v3 on v2

--- a/solution.py
+++ b/solution.py
@@ -52,36 +52,65 @@
     return run
 
 
+def owners(g):
+    even = lax.rem(g, 2) == 0
+    other = jnp.where(even, g + 1, g - 1)
+    return g, other, lax.rem(g + 2, GRP), GRP - 1 - g
+
+
 def images_kernel(
-    info, own0, own1, right0, right1, across0, across1, left0, left1, got,
+    info, own0, own1, side0, side1, across0, across1, back0, back1, got,
     cells, images, blocks_ref, neart_ref, fart_ref, near_ref, far_ref,
     weights, field,
 ):
     g = info[0]
     live = info[1]
     even = info[2] == 0
-    parts = ((own0, own1), (right0, right1), (across0, across1), (left0, left1))
+    parts = ((own0, own1), (side0, side1), (across0, across1), (back0, back1))
+    row_of = owners(g)
     rows = lax.broadcasted_iota(jnp.int32, (CX, CX), 0)
     cols = lax.broadcasted_iota(jnp.int32, (CX, CX), 1)
     gap = jnp.abs(rows - cols)
+    slots = lax.broadcasted_iota(jnp.int32, (SLOTS, CX), 0)
     tri = jnp.where(gap == 0, 1.0, jnp.where(gap == 1, 0.5, 0.0)).astype(F32)
-    for o in range(GRP):
-        for q in range(GRP):
-            dist = jnp.abs(lax.rem(g + o, GRP) - lax.rem(g + q, GRP))
-            coef = jnp.where(dist == 0, 1.0, jnp.where(dist == 1, 0.5, 0.0)).astype(F32)
-            weights[o * CX:(o + 1) * CX, q * CX:(q + 1) * CX] = (tri * coef).astype(BF16)
+    none = jnp.zeros((CX, CX), BF16)
+    weights[...] = jnp.concatenate(
+        [
+            jnp.concatenate([tri.astype(BF16), none], axis=1),
+            jnp.concatenate([none, tri.astype(BF16)], axis=1),
+        ],
+        axis=0,
+    )
+    outer = jnp.where((g == 1) | (g == 2), 0.5, 0.0).astype(F32)
+    inner = 0.5 - outer
     for p in range(PLANES):
         for o in range(GRP):
             plane = parts[o][p // 2][p % 2]
-            cells[:, p * CELLS + o * CX:p * CELLS + (o + 1) * CX] = plane[...]
+            cells[:, p * CELLS + o * CX:p * CELLS + (o + 1) * CX] = jnp.where(
+                slots < live, plane[...].astype(F32), 0.0
+            ).astype(BF16)
     for o in range(GRP):
-        field[:, o * CX:(o + 1) * CX] = 16.0 + got[lax.rem(g + o, GRP), COLS:, :]
+        field[:, o * CX:(o + 1) * CX] = 16.0 + got[row_of[o], COLS:, :]
 
     def slot_half(h, carry):
-        row = pl.ds(pl.multiple_of(h * HALF, HALF), HALF)
+        row = slice(h * HALF, (h + 1) * HALF)
         smooth = []
         for p in range(PLANES):
-            smooth.append(dot(cells[row, p * CELLS:(p + 1) * CELLS], weights[...]))
+            low_pair = dot(cells[row, p * CELLS:p * CELLS + 2 * CX], weights[...])
+            high_pair = dot(cells[row, p * CELLS + 2 * CX:(p + 1) * CELLS], weights[...])
+            s0, s1 = low_pair[:, :CX], low_pair[:, CX:]
+            s2, s3 = high_pair[:, :CX], high_pair[:, CX:]
+            smooth.append(
+                jnp.concatenate(
+                    [
+                        s0 + 0.5 * s1 + outer * s3,
+                        s1 + 0.5 * s0 + inner * s2,
+                        s2 + 0.5 * s3 + inner * s1,
+                        s3 + 0.5 * s2 + outer * s0,
+                    ],
+                    axis=1,
+                )
+            )
         low_plane, high_plane = smooth[0].astype(BF16), smooth[PLANES - 1].astype(BF16)
         near_ref[row, :] = jnp.where(even, high_plane, low_plane)
         far_ref[row, :] = jnp.where(even, low_plane, high_plane)
@@ -98,8 +127,8 @@
                 field[p:p + 1, :] * own - 2.0 * along
             ).astype(BF16)
         for i in range(HALF // BLK):
-            first_slot = pl.multiple_of(h * HALF + i * BLK, BLK)
-            line = pl.ds(first_slot, BLK)
+            first_slot = h * HALF + i * BLK
+            line = slice(first_slot, first_slot + BLK)
             block = dot_last(images[line, :], cells[line, :])
             pad = (gap == 0) & (first_slot + rows >= live)
             blocks_ref[:, line] = 0.5 * (block + block.T) + jnp.where(pad, 1.0, 0.0).astype(F32)
@@ -111,25 +140,8 @@
             fart_ref[c * CX:(c + 1) * CX, row] = jnp.where(even, low_turned, high_turned)
         return carry
 
-    lax.fori_loop(0, SLOTS // HALF, slot_half, 0)
-
-
-def matrix_kernel(info, cells, images, r_ref, d_ref, eh_ref, el_ref, t_ref):
-    live = info[1]
-
-    def slot_half(h, carry):
-        row = pl.ds(pl.multiple_of(h * HALF, HALF), HALF)
-        matrix = dot_last(images[row, :], cells[...])
-        slot = h * HALF + lax.broadcasted_iota(jnp.int32, (HALF, SLOTS), 0)
-        column = lax.broadcasted_iota(jnp.int32, (HALF, SLOTS), 1)
-        matrix = matrix + jnp.where((slot == column) & (slot >= live), 1.0, 0.0).astype(F32)
-        high, low = split(matrix)
-        eh_ref[row, :] = high
-        el_ref[row, :] = low
-        return carry
-
-    lax.fori_loop(0, SLOTS // HALF, slot_half, 0)
-    local_kernel(r_ref, d_ref, eh_ref, el_ref, t_ref)
+    for h in range(SLOTS // HALF):
+        slot_half(h, 0)
 
 
 def invert2(m):
@@ -160,7 +172,8 @@
     )
 
 
-def inverse_kernel(blocks_ref, high_ref, low_ref, work):
+def inverse_kernel(info, blocks_ref, cells, images, high_ref, low_ref, eh_ref, el_ref, work):
+    live = info[1]
     work[...] = blocks_ref[...]
     lane = lax.broadcasted_iota(jnp.int32, (8, BLK), 1)
     sub = lax.broadcasted_iota(jnp.int32, (8, BLK), 0)
@@ -179,18 +192,29 @@
             piece = turn(work[rows, j * BLK:(j + 1) * BLK], j - p)
             packed = piece if packed is None else jnp.where(group == j, piece, packed)
         tiles = [packed[8 * v:8 * v + 8] for v in range(count)]
+        lines = slice(p // 2 * HALF, (p // 2 + 1) * HALF)
+        columns = slice(p % 2 * HALF, (p % 2 + 1) * HALF)
+        matrix = dot_last(images[lines, :], cells[columns, :])
+        if p // 2 == p % 2:
+            slot = lax.broadcasted_iota(jnp.int32, (HALF, HALF), 0)
+            column = lax.broadcasted_iota(jnp.int32, (HALF, HALF), 1)
+            pad = (slot == column) & (slot + p // 2 * HALF >= live)
+            matrix = matrix + jnp.where(pad, 1.0, 0.0).astype(F32)
+        matrix_high, matrix_low = split(matrix)
+        eh_ref[lines, columns] = matrix_high
+        el_ref[lines, columns] = matrix_low
         for k in range(0, PANEL, 4):
             v, q = k // 8, k % 8
             cols = [[jnp.take_along_axis(t, base + (k + c), axis=1) for t in tiles] for c in range(4)]
             pivot = invert4([[spread(cols[c][v], q + i) for c in range(4)] for i in range(4)])
             inside = (within >= k) & (within < k + 4)
-            lines = [
+            pivot_rows = [
                 jnp.where(inside, jnp.where(within == k + i, 1.0, 0.0), spread(tiles[v], q + i))
                 for i in range(4)
             ]
             new = [
-                (pivot[i][0] * lines[0] + pivot[i][1] * lines[1])
-                + (pivot[i][2] * lines[2] + pivot[i][3] * lines[3])
+                (pivot[i][0] * pivot_rows[0] + pivot[i][1] * pivot_rows[1])
+                + (pivot[i][2] * pivot_rows[2] + pivot[i][3] * pivot_rows[3])
                 for i in range(4)
             ]
             for u in range(count):
@@ -273,8 +297,12 @@
     out_ref[...] = x_ref[...] + precondition(residual, ih_ref, il_ref)
 
 
-def shift_by(values, offset):
-    return lax.ppermute(values, "grp", [(i, (i + offset) % GRP) for i in range(GRP)])
+SIDE = ((0, 1), (1, 0), (2, 3), (3, 2))
+BACK = ((0, 3), (3, 0), (1, 2), (2, 1))
+
+
+def swap(values, pairs):
+    return lax.ppermute(values, "grp", pairs)
 
 
 def on_device_steps(deflation, shift_field, counts, right_sides):
@@ -283,21 +311,18 @@
     live_count = counts[0]
     parity = lax.rem(lax.axis_index("sub"), 2)
     info = jnp.stack([g.astype(jnp.int32), live_count, parity.astype(jnp.int32)])
-    slot_ids = lax.iota(jnp.int32, SLOTS)
-    live = slot_ids < live_count
-    masked = jnp.where(live[:, None, None, None], deflation, jnp.zeros((), BF16))
-    planes = jnp.transpose(masked.reshape(SLOTS, PLANES, CX), (1, 0, 2))
+    planes = jnp.transpose(deflation.reshape(SLOTS, PLANES, CX), (1, 0, 2))
     own0, own1 = planes[:2], planes[2:]
     row_slot = g * BLK + lax.iota(jnp.int32, BLK)
     rhs = jnp.where((row_slot >= live_count)[:, None], 0.0, right_sides).T.reshape(GRP, COLS, BLK)
     field = jnp.zeros((8, CX), F32).at[:PLANES].set(shift_field.reshape(PLANES, CX))
     pieces = jnp.concatenate([rhs, jnp.broadcast_to(field, (GRP, 8, CX))], axis=1)
-    left0 = shift_by(own0, 1)
-    right1 = shift_by(own1, -1)
-    left1 = shift_by(own1, 1)
-    right0 = shift_by(own0, -1)
-    across0 = shift_by(left0, 1)
-    across1 = shift_by(right1, -1)
+    side0 = swap(own0, SIDE)
+    back1 = swap(own1, BACK)
+    back0 = swap(own0, BACK)
+    side1 = swap(own1, SIDE)
+    across0 = swap(side0, BACK)
+    across1 = swap(back1, SIDE)
     got = lax.all_to_all(pieces, "grp", 0, 0)
 
     square = (SLOTS, SLOTS)
@@ -305,18 +330,18 @@
     cells, images, blocks, neart, fart, near, far = call(
         images_kernel,
         [(tall, BF16), (tall, BF16), ((BLK, SLOTS), F32)] + [(square, BF16)] * 4,
-        scratch=[pltpu.VMEM((CELLS, CELLS), BF16), pltpu.VMEM((8, CELLS), F32)],
+        scratch=[pltpu.VMEM((2 * CX, 2 * CX), BF16), pltpu.VMEM((8, CELLS), F32)],
         limit=24,
         flops=2 * 10**9,
         nbytes=8 << 20,
-    )(info, own0, own1, right0, right1, across0, across1, left0, left1, got)
-    ih, il = call(
+    )(info, own0, own1, side0, side1, across0, across1, back0, back1, got)
+    ih, il, eh, el = call(
         inverse_kernel,
-        [((BLK, SLOTS), BF16)] * 2,
+        [((BLK, SLOTS), BF16)] * 2 + [(square, BF16)] * 2,
         scratch=[pltpu.VMEM((BLK, SLOTS), F32)],
         flops=10**9,
-        nbytes=1 << 19,
-    )(blocks)
+        nbytes=5 << 20,
+    )(info, blocks, cells, images)
 
     vec = (COLS, SLOTS)
     r, d, near_msg, far_msg = call(
@@ -330,10 +355,7 @@
         far_got = lax.ppermute(far_msg, "sub", far_pairs)
         near_got = lax.ppermute(near_msg, "sub", near_pairs)
         if sweep == 1:
-            eh, el, t = call(
-                matrix_kernel, [(square, BF16), (square, BF16), (vec, F32)],
-                limit=16, flops=10**9, nbytes=5 << 20,
-            )(info, cells, images, r, d)
+            (t,) = call(local_kernel, [(vec, F32)], flops=10**8, nbytes=1 << 20)(r, d, eh, el)
         else:
             t, x = call(
                 both_kernel, [(vec, F32), (vec, F32)], flops=10**8, nbytes=1 << 20,

time: 105 us -> 103 us (0.981)
  Pallas kernels: 18.3 us -> 16.6 us
  other arithmetic: 2.03 us -> 0.85 us
  local copies, waits for them, and re-layouts: 0.91 us -> 2.05 us
    pallas_call x13, Pallas kernels: 18.3 us -> 16.6 us  [run(): pl.pallas_call(kernel, out_shape=[jax.ShapeDtypeStruct(s, d) for s, d in...]
    transpose x1 -> x0, other arithmetic: 1.18 us -> none  [on_device_steps(): planes = jnp.transpose(masked.reshape(SLOTS, PLANES, CX), (1, 0, 2))]
    all_to_all x1, starting transfers between devices: 4.49 us -> 3.33 us  [on_device_steps(): got = lax.all_to_all(pieces, 'grp', 0, 0)]
    unnamed x4 -> x5, local copies, waits for them, and re-layouts: 0.01 us -> 1.15 us
    ppermute x5, starting transfers between devices: 29.7 us -> 30.7 us  [on_device_steps(): far_got = lax.ppermute(far_msg, 'sub', far_pairs)]
  transfers between devices with their start and end apart: 17 -> 17, of which waited for: 5 -> 6; matrix products, arithmetic and copies ran while one was open for 1% -> 1% of each run, Pallas kernels for 3% -> 1%
where the time goes in v3:
time: 103 us
  starting transfers between devices  63.2 us (61%)
  Pallas kernels  16.6 us (16%)
  waiting for transfers between devices  10.5 us (10%)
  blocking collectives  8.36 us (8%)
  local copies, waits for them, and re-layouts  2.05 us (2%)
    ppermute x5, starting transfers between devices, on_device_steps(): far_got = lax.ppermute(far_msg, 'sub', far_pairs)  30.7 us
    ppermute x6, starting transfers between devices, swap(): return lax.ppermute(values, 'grp', pairs)  19.5 us
    pallas_call x13, Pallas kernels, run(): pl.pallas_call(kernel, out_shape=[jax.ShapeDtypeStruct(s, d) for s, d in...  16.6 us
    ppermute x5, starting transfers between devices, on_device_steps(): near_got = lax.ppermute(near_msg, 'sub', near_pairs)  9.6 us
    all_to_all x1, blocking collectives, on_device_steps(): return lax.all_to_all(x, 'grp', 1, 0, tiled=True).T  8.36 us
    all_to_all x1, waiting for transfers between devices, on_device_steps(): got = lax.all_to_all(pieces, 'grp', 0, 0)  5.95 us
    ppermute x5, waiting for transfers between devices, on_device_steps(): far_got = lax.ppermute(far_msg, 'sub', far_pairs)  3.66 us
    all_to_all x1, starting transfers between devices, on_device_steps(): got = lax.all_to_all(pieces, 'grp', 0, 0)  3.33 us
  transfers between devices with their start and end apart: 17, of which 6 were waited for; matrix products, arithmetic and copies ran while one was open for 1% of the time, Pallas kernels for 1%

profile of v3, /device:TPU:32, one launch (start us, length us, event | category | flops | bytes accessed | tf_op | source)
XLA Modules:
  0.0 102.6 jit_solution(12922163997793033058)
XLA Ops:
  0.0 0.0 copy-start
  0.0 0.0 copy-start.1
  0.0 1.1 %copy.15 = bf16[512,4,1,128]{3,0,1,2:T(8,128)(2,1)S(1)} copy(bf16[512,4,1,128]{3,1,2,0:T(4,128)(2,1)} %param.6) | data formatting | bytes 1048576 | tf_op args[0]
  1.2 4.7 %collective-permute-start.3 = (bf16[2,512,128]{2,1,0:T(8,128)(2,1)S(1)}, bf16[2,512,128]{2,1,0:T(8,128)(2,1)S(1)}, u32[]{:S(2)}, u32[]{:S(2)}) collective-permute-start(bf16[2,512,128]{2,1,0:T(8,128)(2,1)S(1)} %get-tuple-element.95.own1), channel_id=1, source_target_pairs={{0,3},{3,0},{1,2},{2,1},{4,7},{7,4},{5,6},{6,5},{8,11},{11,8},{9,1... | collective-permute-start | bytes 786440 | tf_op jit(solution)/shard_map/ppermute | solution.py:305
  5.9 2.1 %collective-permute-start = (bf16[2,512,128]{2,1,0:T(8,128)(2,1)S(1)}, bf16[2,512,128]{2,1,0:T(8,128)(2,1)S(1)}, u32[]{:S(2)}, u32[]{:S(2)}) collective-permute-start(bf16[2,512,128]{2,1,0:T(8,128)(2,1)S(1)} %get-tuple-element.96.own0), channel_id=1, source_target_pairs={{0,1},{1,0},{2,3},{3,2},{4,5},{5,4},{6,7},{7,6},{8,9},{9,8},{10,11... | collective-permute-start | bytes 786440 | tf_op jit(solution)/shard_map/ppermute | solution.py:305
  8.0 3.7 %collective-permute-start.1 = (bf16[2,512,128]{2,1,0:T(8,128)(2,1)S(1)}, bf16[2,512,128]{2,1,0:T(8,128)(2,1)S(1)}, u32[]{:S(2)}, u32[]{:S(2)}) collective-permute-start(bf16[2,512,128]{2,1,0:T(8,128)(2,1)S(1)} %get-tuple-element.95.own1), channel_id=1, source_target_pairs={{0,1},{1,0},{2,3},{3,2},{4,5},{5,4},{6,7},{7,6},{8,9},{9,8},{10,11... | collective-permute-start | bytes 786440 | tf_op jit(solution)/shard_map/ppermute | solution.py:305
  11.7 2.4 %collective-permute-start.5 = (bf16[2,512,128]{2,1,0:T(8,128)(2,1)S(1)}, bf16[2,512,128]{2,1,0:T(8,128)(2,1)S(1)}, u32[]{:S(2)}, u32[]{:S(2)}) collective-permute-start(bf16[2,512,128]{2,1,0:T(8,128)(2,1)S(1)} %get-tuple-element.96.own0), channel_id=1, source_target_pairs={{0,3},{3,0},{1,2},{2,1},{4,7},{7,4},{5,6},{6,5},{8,11},{11,8},{9,1... | collective-permute-start | bytes 786440 | tf_op jit(solution)/shard_map/ppermute | solution.py:305
  14.8 0.0 collective-permute-done.3.back1
  14.8 2.2 %collective-permute-start.4 = (bf16[2,512,128]{2,1,0:T(8,128)(2,1)S(1)}, bf16[2,512,128]{2,1,0:T(8,128)(2,1)S(1)}, u32[]{:S(2)}, u32[]{:S(2)}) collective-permute-start(bf16[2,512,128]{2,1,0:T(8,128)(2,1)S(1)} %collective-permute-done.3.back1), channel_id=1, source_target_pairs={{0,1},{1,0},{2,3},{3,2},{4,5},{5,4},{6,7},{7,6},{8,9},{9,8},{10,11... | collective-permute-start | bytes 786440 | tf_op jit(solution)/shard_map/ppermute | solution.py:305
  17.0 0.0 collective-permute-done.side0
  17.0 4.4 %collective-permute-start.2 = (bf16[2,512,128]{2,1,0:T(8,128)(2,1)S(1)}, bf16[2,512,128]{2,1,0:T(8,128)(2,1)S(1)}, u32[]{:S(2)}, u32[]{:S(2)}) collective-permute-start(bf16[2,512,128]{2,1,0:T(8,128)(2,1)S(1)} %collective-permute-done.side0), channel_id=1, source_target_pairs={{0,3},{3,0},{1,2},{2,1},{4,7},{7,4},{5,6},{6,5},{8,11},{11,8},{9,1... | collective-permute-start | bytes 786440 | tf_op jit(solution)/shard_map/ppermute | solution.py:305
  21.4 0.0 copy-done
  21.4 0.1 select_bitcast_fusion
  21.5 0.1 copy.8
  21.6 0.0 copy-done.1
  21.6 0.7 pad_maximum_fusion
  22.3 3.3 %all-to-all-start = ((f32[4,72,128]{2,1,0:T(8,128)}), f32[4,72,128]{2,1,0:T(8,128)S(1)}, u32[]{:S(2)}, u32[]{:S(2)}) async-start(f32[4,72,128]{2,1,0:T(8,128)} %pad_maximum_fusion), calls=%async_computation | async-start | bytes 294912 | tf_op jit(solution)/shard_map/all_to_all | solution.py:326
  25.7 0.1 pad_add_fusion.info
  25.8 5.9 %all-to-all-done.got = f32[4,72,128]{2,1,0:T(8,128)S(1)} async-done(((f32[4,72,128]{2,1,0:T(8,128)}), f32[4,72,128]{2,1,0:T(8,128)S(1)}, u32[]{:S(2)}, u32[]{:S(2)}) %all-to-all-start) | async-done | bytes 147488 | tf_op jit(solution)/shard_map/all_to_all | solution.py:326
  31.7 0.0 collective-permute-done.1.side1
  31.7 0.0 collective-permute-done.5.back0
  31.7 0.0 collective-permute-done.4.across1
  31.7 0.0 collective-permute-done.2.across0
  31.7 4.0 %shard_map.46 = (bf16[512,2048]{1,0:T(8,128)(2,1)S(1)}, bf16[512,2048]{1,0:T(8,128)(2,1)S(1)}, f32[128,512]{1,0:T(8,128)S(1)}, bf16[512,512]{1,0:T(8,128)(2,1)S(...) custom-call(s32[3]{0:T(128)S(1)} %pad_add_fusion.info, ...), custom_call_target="tpu_custom_call" | custom-call | flops 2000000000 | bytes 8388608 | tf_op jit(solution)/shard_map/pallas_call | solution.py:42
  35.7 7.4 %shard_map.47 = (bf16[128,512]{1,0:T(8,128)(2,1)S(1)}, bf16[128,512]{1,0:T(8,128)(2,1)S(1)}, bf16[512,512]{1,0:T(8,128)(2,1)S(1)}, bf16[512,512]{1,0:T(8,128)(2,1)S(1)}) custom-call(s32[3]{0:T(128)S(1)} %pad_add_fusion.info, f32[128,512]{1,0:T(8,128)S(1)} %get-tuple-element.56.blocks_ref, bf16[512,2048]{1,0:T(8,128)(2,1)S(1)} %get-tuple-element.57.cells, ...), custom_call_target="tpu_custom_call" | custom-call | flops 1000000000 | bytes 5242880 | tf_op jit(solution)/shard_map/pallas_call | solution.py:42
  43.1 0.4 shard_map.48
  43.6 7.7 %collective-permute-start.6 = (bf16[64,512]{1,0:T(8,128)(2,1)S(1)}, bf16[64,512]{1,0:T(8,128)(2,1)S(1)}, u32[]{:S(2)}, u32[]{:S(2)}) collective-permute-start(bf16[64,512]{1,0:T(8,128)(2,1)S(1)} %get-tuple-element.67), channel_id=1, source_target_pairs={{4,8},{8,4},{12,16},{16,12},{20,24},{24,20},{28,32},{32,28},{36,40... | collective-permute-start | bytes 196616 | tf_op jit(solution)/shard_map/ppermute | solution.py:355
  51.3 1.9 %collective-permute-start.7 = (bf16[64,512]{1,0:T(8,128)(2,1)S(1)}, bf16[64,512]{1,0:T(8,128)(2,1)S(1)}, u32[]{:S(2)}, u32[]{:S(2)}) collective-permute-start(bf16[64,512]{1,0:T(8,128)(2,1)S(1)} %get-tuple-element.68), channel_id=1, source_target_pairs={{0,4},{4,0},{8,12},{12,8},{16,20},{20,16},{24,28},{28,24},{32,36},... | collective-permute-start | bytes 196616 | tf_op jit(solution)/shard_map/ppermute | solution.py:356
  53.2 0.3 shard_map.49.t_ref
  53.5 0.0 collective-permute-done.6.far_in
  53.6 0.9 collective-permute-done.7.near_in
  54.5 0.7 shard_map.50
  55.2 5.8 %collective-permute-start.8 = (bf16[64,512]{1,0:T(8,128)(2,1)S(1)}, bf16[64,512]{1,0:T(8,128)(2,1)S(1)}, u32[]{:S(2)}, u32[]{:S(2)}) collective-permute-start(bf16[64,512]{1,0:T(8,128)(2,1)S(1)} %get-tuple-element.74), channel_id=1, source_target_pairs={{4,8},{8,4},{12,16},{16,12},{20,24},{24,20},{28,32},{32,28},{36,40... | collective-permute-start | bytes 196616 | tf_op jit(solution)/shard_map/ppermute | solution.py:355
  60.9 1.9 %collective-permute-start.9 = (bf16[64,512]{1,0:T(8,128)(2,1)S(1)}, bf16[64,512]{1,0:T(8,128)(2,1)S(1)}, u32[]{:S(2)}, u32[]{:S(2)}) collective-permute-start(bf16[64,512]{1,0:T(8,128)(2,1)S(1)} %get-tuple-element.75), channel_id=1, source_target_pairs={{0,4},{4,0},{8,12},{12,8},{16,20},{20,16},{24,28},{28,24},{32,36},... | collective-permute-start | bytes 196616 | tf_op jit(solution)/shard_map/ppermute | solution.py:356
  62.9 0.3 shard_map.51
  63.2 0.9 collective-permute-done.8.far_in
  64.1 0.0 collective-permute-done.9.near_in
  64.1 0.7 shard_map.52
  64.8 5.8 %collective-permute-start.10 = (bf16[64,512]{1,0:T(8,128)(2,1)S(1)}, bf16[64,512]{1,0:T(8,128)(2,1)S(1)}, u32[]{:S(2)}, u32[]{:S(2)}) collective-permute-start(bf16[64,512]{1,0:T(8,128)(2,1)S(1)} %get-tuple-element.80), channel_id=1, source_target_pairs={{4,8},{8,4},{12,16},{16,12},{20,24},{24,20},{28,32},{32,28},{36,40... | collective-permute-start | bytes 196616 | tf_op jit(solution)/shard_map/ppermute | solution.py:355
  70.6 1.9 %collective-permute-start.11 = (bf16[64,512]{1,0:T(8,128)(2,1)S(1)}, bf16[64,512]{1,0:T(8,128)(2,1)S(1)}, u32[]{:S(2)}, u32[]{:S(2)}) collective-permute-start(bf16[64,512]{1,0:T(8,128)(2,1)S(1)} %get-tuple-element.81), channel_id=1, source_target_pairs={{0,4},{4,0},{8,12},{12,8},{16,20},{20,16},{24,28},{28,24},{32,36},... | collective-permute-start | bytes 196616 | tf_op jit(solution)/shard_map/ppermute | solution.py:356
  72.5 0.3 shard_map.53
  72.8 0.9 collective-permute-done.10.far_in
  73.7 0.0 collective-permute-done.11.near_in
  73.7 0.7 shard_map.54
  74.4 5.8 %collective-permute-start.12 = (bf16[64,512]{1,0:T(8,128)(2,1)S(1)}, bf16[64,512]{1,0:T(8,128)(2,1)S(1)}, u32[]{:S(2)}, u32[]{:S(2)}) collective-permute-start(bf16[64,512]{1,0:T(8,128)(2,1)S(1)} %get-tuple-element.86), channel_id=1, source_target_pairs={{4,8},{8,4},{12,16},{16,12},{20,24},{24,20},{28,32},{32,28},{36,40... | collective-permute-start | bytes 196616 | tf_op jit(solution)/shard_map/ppermute | solution.py:355
  80.2 1.9 %collective-permute-start.13 = (bf16[64,512]{1,0:T(8,128)(2,1)S(1)}, bf16[64,512]{1,0:T(8,128)(2,1)S(1)}, u32[]{:S(2)}, u32[]{:S(2)}) collective-permute-start(bf16[64,512]{1,0:T(8,128)(2,1)S(1)} %get-tuple-element.87), channel_id=1, source_target_pairs={{0,4},{4,0},{8,12},{12,8},{16,20},{20,16},{24,28},{28,24},{32,36},... | collective-permute-start | bytes 196616 | tf_op jit(solution)/shard_map/ppermute | solution.py:356
  82.1 0.3 shard_map.55
  82.4 0.9 collective-permute-done.12.far_in
  83.3 0.0 collective-permute-done.13.near_in
  83.3 0.7 shard_map.56
  84.0 5.8 %collective-permute-start.14 = (bf16[64,512]{1,0:T(8,128)(2,1)S(1)}, bf16[64,512]{1,0:T(8,128)(2,1)S(1)}, u32[]{:S(2)}, u32[]{:S(2)}) collective-permute-start(bf16[64,512]{1,0:T(8,128)(2,1)S(1)} %get-tuple-element.93), channel_id=1, source_target_pairs={{4,8},{8,4},{12,16},{16,12},{20,24},{24,20},{28,32},{32,28},{36,40... | collective-permute-start | bytes 196616 | tf_op jit(solution)/shard_map/ppermute | solution.py:355
  89.8 1.9 %collective-permute-start.15 = (bf16[64,512]{1,0:T(8,128)(2,1)S(1)}, bf16[64,512]{1,0:T(8,128)(2,1)S(1)}, u32[]{:S(2)}, u32[]{:S(2)}) collective-permute-start(bf16[64,512]{1,0:T(8,128)(2,1)S(1)} %get-tuple-element.94), channel_id=1, source_target_pairs={{0,4},{4,0},{8,12},{12,8},{16,20},{20,16},{24,28},{28,24},{32,36},... | collective-permute-start | bytes 196616 | tf_op jit(solution)/shard_map/ppermute | solution.py:356
  91.7 0.3 shard_map.57
  92.0 0.9 collective-permute-done.14.far_in
  92.9 0.0 collective-permute-done.15.near_in
  92.9 0.5 shard_map.58
  93.4 8.4 %all_to_all.24 = f32[64,4,128]{2,0,1:T(8,128)S(1)} all-to-all(f32[64,4,128]{2,0,1:T(8,128)S(1)} %copy_bitcast_fusion.1), channel_id=1, replica_groups=mesh['sub'=128,'grp'=4] {'grp'}, dimensions={1} | all-to-all | bytes 262144 | tf_op jit(solution)/shard_map/all_to_all | solution.py:372
  101.8 0.8 copy.11
  (5 shorter events, 0.1 us)
Async XLA Ops:
  0.0 21.4 %copy-start = (f32[128,256]{1,0:T(8,128)S(1)}, f32[128,256]{1,0:T(8,128)}, u32[]{:S(2)}) copy-start(f32[128,256]{1,0:T(8,128)} %param.9) | copy-start | bytes 393220
  0.0 21.6 %copy-start.1 = (f32[4,1,128]{2,1,0:T(1,128)S(1)}, f32[4,1,128]{2,1,0:T(1,128)}, u32[]{:S(2)}) copy-start(f32[4,1,128]{2,1,0:T(1,128)} %param.7) | copy-start | bytes 6148
  1.2 13.6 %collective-permute-start.3 = (bf16[2,512,128]{2,1,0:T(8,128)(2,1)S(1)}, bf16[2,512,128]{2,1,0:T(8,128)(2,1)S(1)}, u32[]{:S(2)}, u32[]{:S(2)}) collective-permute-start(bf16[2,512,128]{2,1,0:T(8,128)(2,1)S(1)} %get-tuple-element.95.own1), channel_id=1, source_target_pairs={{0,3},{3,0},{1,2},{2,1},{4,7},{7,4},{5,6},{6,5},{8,11},{11,8},{9,1... | collective-permute-start | bytes 786440 | tf_op jit(solution)/shard_map/ppermute | solution.py:305
  5.9 11.1 %collective-permute-start = (bf16[2,512,128]{2,1,0:T(8,128)(2,1)S(1)}, bf16[2,512,128]{2,1,0:T(8,128)(2,1)S(1)}, u32[]{:S(2)}, u32[]{:S(2)}) collective-permute-start(bf16[2,512,128]{2,1,0:T(8,128)(2,1)S(1)} %get-tuple-element.96.own0), channel_id=1, source_target_pairs={{0,1},{1,0},{2,3},{3,2},{4,5},{5,4},{6,7},{7,6},{8,9},{9,8},{10,11... | collective-permute-start | bytes 786440 | tf_op jit(solution)/shard_map/ppermute | solution.py:305
  8.0 23.7 %collective-permute-start.1 = (bf16[2,512,128]{2,1,0:T(8,128)(2,1)S(1)}, bf16[2,512,128]{2,1,0:T(8,128)(2,1)S(1)}, u32[]{:S(2)}, u32[]{:S(2)}) collective-permute-start(bf16[2,512,128]{2,1,0:T(8,128)(2,1)S(1)} %get-tuple-element.95.own1), channel_id=1, source_target_pairs={{0,1},{1,0},{2,3},{3,2},{4,5},{5,4},{6,7},{7,6},{8,9},{9,8},{10,11... | collective-permute-start | bytes 786440 | tf_op jit(solution)/shard_map/ppermute | solution.py:305
  11.7 20.0 %collective-permute-start.5 = (bf16[2,512,128]{2,1,0:T(8,128)(2,1)S(1)}, bf16[2,512,128]{2,1,0:T(8,128)(2,1)S(1)}, u32[]{:S(2)}, u32[]{:S(2)}) collective-permute-start(bf16[2,512,128]{2,1,0:T(8,128)(2,1)S(1)} %get-tuple-element.96.own0), channel_id=1, source_target_pairs={{0,3},{3,0},{1,2},{2,1},{4,7},{7,4},{5,6},{6,5},{8,11},{11,8},{9,1... | collective-permute-start | bytes 786440 | tf_op jit(solution)/shard_map/ppermute | solution.py:305
  14.8 16.9 %collective-permute-start.4 = (bf16[2,512,128]{2,1,0:T(8,128)(2,1)S(1)}, bf16[2,512,128]{2,1,0:T(8,128)(2,1)S(1)}, u32[]{:S(2)}, u32[]{:S(2)}) collective-permute-start(bf16[2,512,128]{2,1,0:T(8,128)(2,1)S(1)} %collective-permute-done.3.back1), channel_id=1, source_target_pairs={{0,1},{1,0},{2,3},{3,2},{4,5},{5,4},{6,7},{7,6},{8,9},{9,8},{10,11... | collective-permute-start | bytes 786440 | tf_op jit(solution)/shard_map/ppermute | solution.py:305
  17.0 14.7 %collective-permute-start.2 = (bf16[2,512,128]{2,1,0:T(8,128)(2,1)S(1)}, bf16[2,512,128]{2,1,0:T(8,128)(2,1)S(1)}, u32[]{:S(2)}, u32[]{:S(2)}) collective-permute-start(bf16[2,512,128]{2,1,0:T(8,128)(2,1)S(1)} %collective-permute-done.side0), channel_id=1, source_target_pairs={{0,3},{3,0},{1,2},{2,1},{4,7},{7,4},{5,6},{6,5},{8,11},{11,8},{9,1... | collective-permute-start | bytes 786440 | tf_op jit(solution)/shard_map/ppermute | solution.py:305
  22.3 9.4 %all-to-all-start = ((f32[4,72,128]{2,1,0:T(8,128)}), f32[4,72,128]{2,1,0:T(8,128)S(1)}, u32[]{:S(2)}, u32[]{:S(2)}) async-start(f32[4,72,128]{2,1,0:T(8,128)} %pad_maximum_fusion), calls=%async_computation | async-start | bytes 294912 | tf_op jit(solution)/shard_map/all_to_all | solution.py:326
  43.6 10.0 %collective-permute-start.6 = (bf16[64,512]{1,0:T(8,128)(2,1)S(1)}, bf16[64,512]{1,0:T(8,128)(2,1)S(1)}, u32[]{:S(2)}, u32[]{:S(2)}) collective-permute-start(bf16[64,512]{1,0:T(8,128)(2,1)S(1)} %get-tuple-element.67), channel_id=1, source_target_pairs={{4,8},{8,4},{12,16},{16,12},{20,24},{24,20},{28,32},{32,28},{36,40... | collective-permute-start | bytes 196616 | tf_op jit(solution)/shard_map/ppermute | solution.py:355
  51.3 3.1 %collective-permute-start.7 = (bf16[64,512]{1,0:T(8,128)(2,1)S(1)}, bf16[64,512]{1,0:T(8,128)(2,1)S(1)}, u32[]{:S(2)}, u32[]{:S(2)}) collective-permute-start(bf16[64,512]{1,0:T(8,128)(2,1)S(1)} %get-tuple-element.68), channel_id=1, source_target_pairs={{0,4},{4,0},{8,12},{12,8},{16,20},{20,16},{24,28},{28,24},{32,36},... | collective-permute-start | bytes 196616 | tf_op jit(solution)/shard_map/ppermute | solution.py:356
  55.2 8.9 %collective-permute-start.8 = (bf16[64,512]{1,0:T(8,128)(2,1)S(1)}, bf16[64,512]{1,0:T(8,128)(2,1)S(1)}, u32[]{:S(2)}, u32[]{:S(2)}) collective-permute-start(bf16[64,512]{1,0:T(8,128)(2,1)S(1)} %get-tuple-element.74), channel_id=1, source_target_pairs={{4,8},{8,4},{12,16},{16,12},{20,24},{24,20},{28,32},{32,28},{36,40... | collective-permute-start | bytes 196616 | tf_op jit(solution)/shard_map/ppermute | solution.py:355
  60.9 3.1 %collective-permute-start.9 = (bf16[64,512]{1,0:T(8,128)(2,1)S(1)}, bf16[64,512]{1,0:T(8,128)(2,1)S(1)}, u32[]{:S(2)}, u32[]{:S(2)}) collective-permute-start(bf16[64,512]{1,0:T(8,128)(2,1)S(1)} %get-tuple-element.75), channel_id=1, source_target_pairs={{0,4},{4,0},{8,12},{12,8},{16,20},{20,16},{24,28},{28,24},{32,36},... | collective-permute-start | bytes 196616 | tf_op jit(solution)/shard_map/ppermute | solution.py:356
  64.8 8.9 %collective-permute-start.10 = (bf16[64,512]{1,0:T(8,128)(2,1)S(1)}, bf16[64,512]{1,0:T(8,128)(2,1)S(1)}, u32[]{:S(2)}, u32[]{:S(2)}) collective-permute-start(bf16[64,512]{1,0:T(8,128)(2,1)S(1)} %get-tuple-element.80), channel_id=1, source_target_pairs={{4,8},{8,4},{12,16},{16,12},{20,24},{24,20},{28,32},{32,28},{36,40... | collective-permute-start | bytes 196616 | tf_op jit(solution)/shard_map/ppermute | solution.py:355
  70.6 3.1 %collective-permute-start.11 = (bf16[64,512]{1,0:T(8,128)(2,1)S(1)}, bf16[64,512]{1,0:T(8,128)(2,1)S(1)}, u32[]{:S(2)}, u32[]{:S(2)}) collective-permute-start(bf16[64,512]{1,0:T(8,128)(2,1)S(1)} %get-tuple-element.81), channel_id=1, source_target_pairs={{0,4},{4,0},{8,12},{12,8},{16,20},{20,16},{24,28},{28,24},{32,36},... | collective-permute-start | bytes 196616 | tf_op jit(solution)/shard_map/ppermute | solution.py:356
  74.4 8.9 %collective-permute-start.12 = (bf16[64,512]{1,0:T(8,128)(2,1)S(1)}, bf16[64,512]{1,0:T(8,128)(2,1)S(1)}, u32[]{:S(2)}, u32[]{:S(2)}) collective-permute-start(bf16[64,512]{1,0:T(8,128)(2,1)S(1)} %get-tuple-element.86), channel_id=1, source_target_pairs={{4,8},{8,4},{12,16},{16,12},{20,24},{24,20},{28,32},{32,28},{36,40... | collective-permute-start | bytes 196616 | tf_op jit(solution)/shard_map/ppermute | solution.py:355
  80.2 3.1 %collective-permute-start.13 = (bf16[64,512]{1,0:T(8,128)(2,1)S(1)}, bf16[64,512]{1,0:T(8,128)(2,1)S(1)}, u32[]{:S(2)}, u32[]{:S(2)}) collective-permute-start(bf16[64,512]{1,0:T(8,128)(2,1)S(1)} %get-tuple-element.87), channel_id=1, source_target_pairs={{0,4},{4,0},{8,12},{12,8},{16,20},{20,16},{24,28},{28,24},{32,36},... | collective-permute-start | bytes 196616 | tf_op jit(solution)/shard_map/ppermute | solution.py:356
  84.0 8.9 %collective-permute-start.14 = (bf16[64,512]{1,0:T(8,128)(2,1)S(1)}, bf16[64,512]{1,0:T(8,128)(2,1)S(1)}, u32[]{:S(2)}, u32[]{:S(2)}) collective-permute-start(bf16[64,512]{1,0:T(8,128)(2,1)S(1)} %get-tuple-element.93), channel_id=1, source_target_pairs={{4,8},{8,4},{12,16},{16,12},{20,24},{24,20},{28,32},{32,28},{36,40... | collective-permute-start | bytes 196616 | tf_op jit(solution)/shard_map/ppermute | solution.py:355
  89.8 3.1 %collective-permute-start.15 = (bf16[64,512]{1,0:T(8,128)(2,1)S(1)}, bf16[64,512]{1,0:T(8,128)(2,1)S(1)}, u32[]{:S(2)}, u32[]{:S(2)}) collective-permute-start(bf16[64,512]{1,0:T(8,128)(2,1)S(1)} %get-tuple-element.94), channel_id=1, source_target_pairs={{0,4},{4,0},{8,12},{12,8},{16,20},{20,16},{24,28},{28,24},{32,36},... | collective-permute-start | bytes 196616 | tf_op jit(solution)/shard_map/ppermute | solution.py:356

commit v4 on v3

--- a/solution.py
+++ b/solution.py
@@ -60,7 +60,7 @@
 
 def images_kernel(
     info, own0, own1, side0, side1, across0, across1, back0, back1, got,
-    cells, images, blocks_ref, neart_ref, fart_ref, near_ref, far_ref,
+    cells, images, blocks_ref, diag_ref, neart_ref, fart_ref, near_ref, far_ref,
     weights, field,
 ):
     g = info[0]
@@ -126,12 +126,15 @@
             images[row, p * CELLS:(p + 1) * CELLS] = (
                 field[p:p + 1, :] * own - 2.0 * along
             ).astype(BF16)
+        quarter = dot_last(images[row, :], cells[row, :])
+        slot = lax.broadcasted_iota(jnp.int32, (HALF, HALF), 0)
+        column = lax.broadcasted_iota(jnp.int32, (HALF, HALF), 1)
+        pad = (slot == column) & (slot + h * HALF >= live)
+        quarter = quarter + jnp.where(pad, 1.0, 0.0).astype(F32)
+        diag_ref[:, row] = quarter
         for i in range(HALF // BLK):
-            first_slot = h * HALF + i * BLK
-            line = slice(first_slot, first_slot + BLK)
-            block = dot_last(images[line, :], cells[line, :])
-            pad = (gap == 0) & (first_slot + rows >= live)
-            blocks_ref[:, line] = 0.5 * (block + block.T) + jnp.where(pad, 1.0, 0.0).astype(F32)
+            block = quarter[i * BLK:(i + 1) * BLK, i * BLK:(i + 1) * BLK]
+            blocks_ref[:, h * HALF + i * BLK:h * HALF + (i + 1) * BLK] = 0.5 * (block + block.T)
         for c in range(GRP):
             first = (PLANES - 1) * CELLS + c * CX
             low_turned = cells[row, c * CX:(c + 1) * CX].astype(F32).T.astype(BF16)
@@ -172,8 +175,7 @@
     )
 
 
-def inverse_kernel(info, blocks_ref, cells, images, high_ref, low_ref, eh_ref, el_ref, work):
-    live = info[1]
+def inverse_kernel(blocks_ref, diag_ref, cells, images, high_ref, low_ref, eh_ref, el_ref, work):
     work[...] = blocks_ref[...]
     lane = lax.broadcasted_iota(jnp.int32, (8, BLK), 1)
     sub = lax.broadcasted_iota(jnp.int32, (8, BLK), 0)
@@ -194,12 +196,10 @@
         tiles = [packed[8 * v:8 * v + 8] for v in range(count)]
         lines = slice(p // 2 * HALF, (p // 2 + 1) * HALF)
         columns = slice(p % 2 * HALF, (p % 2 + 1) * HALF)
-        matrix = dot_last(images[lines, :], cells[columns, :])
         if p // 2 == p % 2:
-            slot = lax.broadcasted_iota(jnp.int32, (HALF, HALF), 0)
-            column = lax.broadcasted_iota(jnp.int32, (HALF, HALF), 1)
-            pad = (slot == column) & (slot + p // 2 * HALF >= live)
-            matrix = matrix + jnp.where(pad, 1.0, 0.0).astype(F32)
+            matrix = diag_ref[:, columns]
+        else:
+            matrix = dot_last(images[lines, :], cells[columns, :])
         matrix_high, matrix_low = split(matrix)
         eh_ref[lines, columns] = matrix_high
         el_ref[lines, columns] = matrix_low
@@ -327,9 +327,10 @@
 
     square = (SLOTS, SLOTS)
     tall = (SLOTS, PLANES * CELLS)
-    cells, images, blocks, neart, fart, near, far = call(
+    cells, images, blocks, diag, neart, fart, near, far = call(
         images_kernel,
-        [(tall, BF16), (tall, BF16), ((BLK, SLOTS), F32)] + [(square, BF16)] * 4,
+        [(tall, BF16), (tall, BF16), ((BLK, SLOTS), F32), ((HALF, SLOTS), F32)]
+        + [(square, BF16)] * 4,
         scratch=[pltpu.VMEM((2 * CX, 2 * CX), BF16), pltpu.VMEM((8, CELLS), F32)],
         limit=24,
         flops=2 * 10**9,
@@ -341,7 +342,7 @@
         scratch=[pltpu.VMEM((BLK, SLOTS), F32)],
         flops=10**9,
         nbytes=5 << 20,
-    )(info, blocks, cells, images)
+    )(blocks, diag, cells, images)
 
     vec = (COLS, SLOTS)
     r, d, near_msg, far_msg = call(

time: 103 us -> 103 us (level)
  no operation moved by 1% of the time
where the time goes in v4:
time: 103 us; the launch traced here: 102 us
  starting transfers between devices  63.2 us (61%)
  Pallas kernels  16 us (16%)
  waiting for transfers between devices  10.6 us (10%)
  blocking collectives  8.36 us (8%)
  local copies, waits for them, and re-layouts  2.05 us (2%)
    ppermute x5, starting transfers between devices, on_device_steps(): far_got = lax.ppermute(far_msg, 'sub', far_pairs)  30.7 us
    ppermute x6, starting transfers between devices, swap(): return lax.ppermute(values, 'grp', pairs)  19.5 us
    pallas_call x13, Pallas kernels, run(): pl.pallas_call(kernel, out_shape=[jax.ShapeDtypeStruct(s, d) for s, d in...  16 us
    ppermute x5, starting transfers between devices, on_device_steps(): near_got = lax.ppermute(near_msg, 'sub', near_pairs)  9.6 us
    all_to_all x1, blocking collectives, on_device_steps(): return lax.all_to_all(x, 'grp', 1, 0, tiled=True).T  8.36 us
    all_to_all x1, waiting for transfers between devices, on_device_steps(): got = lax.all_to_all(pieces, 'grp', 0, 0)  5.95 us
    ppermute x5, waiting for transfers between devices, on_device_steps(): far_got = lax.ppermute(far_msg, 'sub', far_pairs)  3.69 us
    all_to_all x1, starting transfers between devices, on_device_steps(): got = lax.all_to_all(pieces, 'grp', 0, 0)  3.33 us
  transfers between devices with their start and end apart: 17, of which 6 were waited for; matrix products, arithmetic and copies ran while one was open for 1% of the time, Pallas kernels for 1%

profile of v4, /device:TPU:32, one launch (start us, length us, event | category | flops | bytes accessed | tf_op | source)
XLA Modules:
  0.0 102.0 jit_solution(10174833387743977639)
XLA Ops:
  0.0 0.0 copy-start
  0.0 0.0 copy-start.1
  0.0 1.1 %copy.15 = bf16[512,4,1,128]{3,0,1,2:T(8,128)(2,1)S(1)} copy(bf16[512,4,1,128]{3,1,2,0:T(4,128)(2,1)} %param.6) | data formatting | bytes 1048576 | tf_op args[0]
  1.2 4.7 %collective-permute-start.3 = (bf16[2,512,128]{2,1,0:T(8,128)(2,1)S(1)}, bf16[2,512,128]{2,1,0:T(8,128)(2,1)S(1)}, u32[]{:S(2)}, u32[]{:S(2)}) collective-permute-start(bf16[2,512,128]{2,1,0:T(8,128)(2,1)S(1)} %get-tuple-element.97.own1), channel_id=1, source_target_pairs={{0,3},{3,0},{1,2},{2,1},{4,7},{7,4},{5,6},{6,5},{8,11},{11,8},{9,1... | collective-permute-start | bytes 786440 | tf_op jit(solution)/shard_map/ppermute | solution.py:305
  5.9 2.1 %collective-permute-start = (bf16[2,512,128]{2,1,0:T(8,128)(2,1)S(1)}, bf16[2,512,128]{2,1,0:T(8,128)(2,1)S(1)}, u32[]{:S(2)}, u32[]{:S(2)}) collective-permute-start(bf16[2,512,128]{2,1,0:T(8,128)(2,1)S(1)} %get-tuple-element.98.own0), channel_id=1, source_target_pairs={{0,1},{1,0},{2,3},{3,2},{4,5},{5,4},{6,7},{7,6},{8,9},{9,8},{10,11... | collective-permute-start | bytes 786440 | tf_op jit(solution)/shard_map/ppermute | solution.py:305
  8.0 3.7 %collective-permute-start.1 = (bf16[2,512,128]{2,1,0:T(8,128)(2,1)S(1)}, bf16[2,512,128]{2,1,0:T(8,128)(2,1)S(1)}, u32[]{:S(2)}, u32[]{:S(2)}) collective-permute-start(bf16[2,512,128]{2,1,0:T(8,128)(2,1)S(1)} %get-tuple-element.97.own1), channel_id=1, source_target_pairs={{0,1},{1,0},{2,3},{3,2},{4,5},{5,4},{6,7},{7,6},{8,9},{9,8},{10,11... | collective-permute-start | bytes 786440 | tf_op jit(solution)/shard_map/ppermute | solution.py:305
  11.7 2.4 %collective-permute-start.5 = (bf16[2,512,128]{2,1,0:T(8,128)(2,1)S(1)}, bf16[2,512,128]{2,1,0:T(8,128)(2,1)S(1)}, u32[]{:S(2)}, u32[]{:S(2)}) collective-permute-start(bf16[2,512,128]{2,1,0:T(8,128)(2,1)S(1)} %get-tuple-element.98.own0), channel_id=1, source_target_pairs={{0,3},{3,0},{1,2},{2,1},{4,7},{7,4},{5,6},{6,5},{8,11},{11,8},{9,1... | collective-permute-start | bytes 786440 | tf_op jit(solution)/shard_map/ppermute | solution.py:305
  14.8 0.0 collective-permute-done.3.back1
  14.8 2.2 %collective-permute-start.4 = (bf16[2,512,128]{2,1,0:T(8,128)(2,1)S(1)}, bf16[2,512,128]{2,1,0:T(8,128)(2,1)S(1)}, u32[]{:S(2)}, u32[]{:S(2)}) collective-permute-start(bf16[2,512,128]{2,1,0:T(8,128)(2,1)S(1)} %collective-permute-done.3.back1), channel_id=1, source_target_pairs={{0,1},{1,0},{2,3},{3,2},{4,5},{5,4},{6,7},{7,6},{8,9},{9,8},{10,11... | collective-permute-start | bytes 786440 | tf_op jit(solution)/shard_map/ppermute | solution.py:305
  17.0 0.0 collective-permute-done.side0
  17.0 4.4 %collective-permute-start.2 = (bf16[2,512,128]{2,1,0:T(8,128)(2,1)S(1)}, bf16[2,512,128]{2,1,0:T(8,128)(2,1)S(1)}, u32[]{:S(2)}, u32[]{:S(2)}) collective-permute-start(bf16[2,512,128]{2,1,0:T(8,128)(2,1)S(1)} %collective-permute-done.side0), channel_id=1, source_target_pairs={{0,3},{3,0},{1,2},{2,1},{4,7},{7,4},{5,6},{6,5},{8,11},{11,8},{9,1... | collective-permute-start | bytes 786440 | tf_op jit(solution)/shard_map/ppermute | solution.py:305
  21.4 0.0 copy-done
  21.4 0.1 select_bitcast_fusion
  21.5 0.1 copy.8
  21.6 0.0 copy-done.1
  21.6 0.7 pad_maximum_fusion
  22.3 3.3 %all-to-all-start = ((f32[4,72,128]{2,1,0:T(8,128)}), f32[4,72,128]{2,1,0:T(8,128)S(1)}, u32[]{:S(2)}, u32[]{:S(2)}) async-start(f32[4,72,128]{2,1,0:T(8,128)} %pad_maximum_fusion), calls=%async_computation | async-start | bytes 294912 | tf_op jit(solution)/shard_map/all_to_all | solution.py:326
  25.7 0.1 pad_add_fusion.info
  25.8 5.9 %all-to-all-done.got = f32[4,72,128]{2,1,0:T(8,128)S(1)} async-done(((f32[4,72,128]{2,1,0:T(8,128)}), f32[4,72,128]{2,1,0:T(8,128)S(1)}, u32[]{:S(2)}, u32[]{:S(2)}) %all-to-all-start) | async-done | bytes 147488 | tf_op jit(solution)/shard_map/all_to_all | solution.py:326
  31.7 0.0 collective-permute-done.1.side1
  31.7 0.0 collective-permute-done.5.back0
  31.7 0.0 collective-permute-done.4.across1
  31.7 0.0 collective-permute-done.2.across0
  31.7 4.0 %shard_map.46 = (bf16[512,2048]{1,0:T(8,128)(2,1)S(1)}, bf16[512,2048]{1,0:T(8,128)(2,1)S(1)}, f32[128,512]{1,0:T(8,128)S(1)}, f32[256,512]{1,0:T(8,128)S(1)}, b...) custom-call(s32[3]{0:T(128)S(1)} %pad_add_fusion.info, ...), custom_call_target="tpu_custom_call" | custom-call | flops 2000000000 | bytes 8388608 | tf_op jit(solution)/shard_map/pallas_call | solution.py:42
  35.8 6.8 %shard_map.47 = (bf16[128,512]{1,0:T(8,128)(2,1)S(1)}, bf16[128,512]{1,0:T(8,128)(2,1)S(1)}, bf16[512,512]{1,0:T(8,128)(2,1)S(1)}, bf16[512,512]{1,0:T(8,128)(2,1)S(1)}) custom-call(f32[128,512]{1,0:T(8,128)S(1)} %get-tuple-element.57.blocks_ref, f32[256,512]{1,0:T(8,128)S(1)} %get-tuple-element.58.diag_ref, bf16[512,2048]{1,0:T(8,128)(2,1)S(1)} %get-tuple-element.59.cells, ...), custom_call_target="tpu_custom_call" | custom-call | flops 1000000000 | bytes 5242880 | tf_op jit(solution)/shard_map/pallas_call | solution.py:42
  42.6 0.4 shard_map.48
  43.1 7.7 %collective-permute-start.6 = (bf16[64,512]{1,0:T(8,128)(2,1)S(1)}, bf16[64,512]{1,0:T(8,128)(2,1)S(1)}, u32[]{:S(2)}, u32[]{:S(2)}) collective-permute-start(bf16[64,512]{1,0:T(8,128)(2,1)S(1)} %get-tuple-element.69), channel_id=1, source_target_pairs={{4,8},{8,4},{12,16},{16,12},{20,24},{24,20},{28,32},{32,28},{36,40... | collective-permute-start | bytes 196616 | tf_op jit(solution)/shard_map/ppermute | solution.py:356
  50.8 1.9 %collective-permute-start.7 = (bf16[64,512]{1,0:T(8,128)(2,1)S(1)}, bf16[64,512]{1,0:T(8,128)(2,1)S(1)}, u32[]{:S(2)}, u32[]{:S(2)}) collective-permute-start(bf16[64,512]{1,0:T(8,128)(2,1)S(1)} %get-tuple-element.70), channel_id=1, source_target_pairs={{0,4},{4,0},{8,12},{12,8},{16,20},{20,16},{24,28},{28,24},{32,36},... | collective-permute-start | bytes 196616 | tf_op jit(solution)/shard_map/ppermute | solution.py:357
  52.7 0.3 shard_map.49.t_ref
  53.0 0.0 collective-permute-done.6.far_in
  53.0 0.9 collective-permute-done.7.near_in
  53.9 0.7 shard_map.50
  54.6 5.8 %collective-permute-start.8 = (bf16[64,512]{1,0:T(8,128)(2,1)S(1)}, bf16[64,512]{1,0:T(8,128)(2,1)S(1)}, u32[]{:S(2)}, u32[]{:S(2)}) collective-permute-start(bf16[64,512]{1,0:T(8,128)(2,1)S(1)} %get-tuple-element.76), channel_id=1, source_target_pairs={{4,8},{8,4},{12,16},{16,12},{20,24},{24,20},{28,32},{32,28},{36,40... | collective-permute-start | bytes 196616 | tf_op jit(solution)/shard_map/ppermute | solution.py:356
  60.4 1.9 %collective-permute-start.9 = (bf16[64,512]{1,0:T(8,128)(2,1)S(1)}, bf16[64,512]{1,0:T(8,128)(2,1)S(1)}, u32[]{:S(2)}, u32[]{:S(2)}) collective-permute-start(bf16[64,512]{1,0:T(8,128)(2,1)S(1)} %get-tuple-element.77), channel_id=1, source_target_pairs={{0,4},{4,0},{8,12},{12,8},{16,20},{20,16},{24,28},{28,24},{32,36},... | collective-permute-start | bytes 196616 | tf_op jit(solution)/shard_map/ppermute | solution.py:357
  62.3 0.3 shard_map.51
  62.6 0.9 collective-permute-done.8.far_in
  63.6 0.0 collective-permute-done.9.near_in
  63.6 0.7 shard_map.52
  64.3 5.8 %collective-permute-start.10 = (bf16[64,512]{1,0:T(8,128)(2,1)S(1)}, bf16[64,512]{1,0:T(8,128)(2,1)S(1)}, u32[]{:S(2)}, u32[]{:S(2)}) collective-permute-start(bf16[64,512]{1,0:T(8,128)(2,1)S(1)} %get-tuple-element.82), channel_id=1, source_target_pairs={{4,8},{8,4},{12,16},{16,12},{20,24},{24,20},{28,32},{32,28},{36,40... | collective-permute-start | bytes 196616 | tf_op jit(solution)/shard_map/ppermute | solution.py:356
  70.0 1.9 %collective-permute-start.11 = (bf16[64,512]{1,0:T(8,128)(2,1)S(1)}, bf16[64,512]{1,0:T(8,128)(2,1)S(1)}, u32[]{:S(2)}, u32[]{:S(2)}) collective-permute-start(bf16[64,512]{1,0:T(8,128)(2,1)S(1)} %get-tuple-element.83), channel_id=1, source_target_pairs={{0,4},{4,0},{8,12},{12,8},{16,20},{20,16},{24,28},{28,24},{32,36},... | collective-permute-start | bytes 196616 | tf_op jit(solution)/shard_map/ppermute | solution.py:357
  72.0 0.3 shard_map.53
  72.3 0.9 collective-permute-done.10.far_in
  73.2 0.0 collective-permute-done.11.near_in
  73.2 0.7 shard_map.54
  73.9 5.8 %collective-permute-start.12 = (bf16[64,512]{1,0:T(8,128)(2,1)S(1)}, bf16[64,512]{1,0:T(8,128)(2,1)S(1)}, u32[]{:S(2)}, u32[]{:S(2)}) collective-permute-start(bf16[64,512]{1,0:T(8,128)(2,1)S(1)} %get-tuple-element.88), channel_id=1, source_target_pairs={{4,8},{8,4},{12,16},{16,12},{20,24},{24,20},{28,32},{32,28},{36,40... | collective-permute-start | bytes 196616 | tf_op jit(solution)/shard_map/ppermute | solution.py:356
  79.6 1.9 %collective-permute-start.13 = (bf16[64,512]{1,0:T(8,128)(2,1)S(1)}, bf16[64,512]{1,0:T(8,128)(2,1)S(1)}, u32[]{:S(2)}, u32[]{:S(2)}) collective-permute-start(bf16[64,512]{1,0:T(8,128)(2,1)S(1)} %get-tuple-element.89), channel_id=1, source_target_pairs={{0,4},{4,0},{8,12},{12,8},{16,20},{20,16},{24,28},{28,24},{32,36},... | collective-permute-start | bytes 196616 | tf_op jit(solution)/shard_map/ppermute | solution.py:357
  81.6 0.3 shard_map.55
  81.9 0.9 collective-permute-done.12.far_in
  82.8 0.0 collective-permute-done.13.near_in
  82.8 0.7 shard_map.56
  83.5 5.8 %collective-permute-start.14 = (bf16[64,512]{1,0:T(8,128)(2,1)S(1)}, bf16[64,512]{1,0:T(8,128)(2,1)S(1)}, u32[]{:S(2)}, u32[]{:S(2)}) collective-permute-start(bf16[64,512]{1,0:T(8,128)(2,1)S(1)} %get-tuple-element.95), channel_id=1, source_target_pairs={{4,8},{8,4},{12,16},{16,12},{20,24},{24,20},{28,32},{32,28},{36,40... | collective-permute-start | bytes 196616 | tf_op jit(solution)/shard_map/ppermute | solution.py:356
  89.3 1.9 %collective-permute-start.15 = (bf16[64,512]{1,0:T(8,128)(2,1)S(1)}, bf16[64,512]{1,0:T(8,128)(2,1)S(1)}, u32[]{:S(2)}, u32[]{:S(2)}) collective-permute-start(bf16[64,512]{1,0:T(8,128)(2,1)S(1)} %get-tuple-element.96), channel_id=1, source_target_pairs={{0,4},{4,0},{8,12},{12,8},{16,20},{20,16},{24,28},{28,24},{32,36},... | collective-permute-start | bytes 196616 | tf_op jit(solution)/shard_map/ppermute | solution.py:357
  91.2 0.3 shard_map.57
  91.5 0.9 collective-permute-done.14.far_in
  92.4 0.0 collective-permute-done.15.near_in
  92.4 0.5 shard_map.58
  92.9 8.4 %all_to_all.24 = f32[64,4,128]{2,0,1:T(8,128)S(1)} all-to-all(f32[64,4,128]{2,0,1:T(8,128)S(1)} %copy_bitcast_fusion.1), channel_id=1, replica_groups=mesh['sub'=128,'grp'=4] {'grp'}, dimensions={1} | all-to-all | bytes 262144 | tf_op jit(solution)/shard_map/all_to_all | solution.py:373
  101.3 0.8 copy.11
  (5 shorter events, 0.1 us)
Async XLA Ops:
  0.0 21.4 %copy-start = (f32[128,256]{1,0:T(8,128)S(1)}, f32[128,256]{1,0:T(8,128)}, u32[]{:S(2)}) copy-start(f32[128,256]{1,0:T(8,128)} %param.9) | copy-start | bytes 393220
  0.0 21.6 %copy-start.1 = (f32[4,1,128]{2,1,0:T(1,128)S(1)}, f32[4,1,128]{2,1,0:T(1,128)}, u32[]{:S(2)}) copy-start(f32[4,1,128]{2,1,0:T(1,128)} %param.7) | copy-start | bytes 6148
  1.2 13.6 %collective-permute-start.3 = (bf16[2,512,128]{2,1,0:T(8,128)(2,1)S(1)}, bf16[2,512,128]{2,1,0:T(8,128)(2,1)S(1)}, u32[]{:S(2)}, u32[]{:S(2)}) collective-permute-start(bf16[2,512,128]{2,1,0:T(8,128)(2,1)S(1)} %get-tuple-element.97.own1), channel_id=1, source_target_pairs={{0,3},{3,0},{1,2},{2,1},{4,7},{7,4},{5,6},{6,5},{8,11},{11,8},{9,1... | collective-permute-start | bytes 786440 | tf_op jit(solution)/shard_map/ppermute | solution.py:305
  5.9 11.1 %collective-permute-start = (bf16[2,512,128]{2,1,0:T(8,128)(2,1)S(1)}, bf16[2,512,128]{2,1,0:T(8,128)(2,1)S(1)}, u32[]{:S(2)}, u32[]{:S(2)}) collective-permute-start(bf16[2,512,128]{2,1,0:T(8,128)(2,1)S(1)} %get-tuple-element.98.own0), channel_id=1, source_target_pairs={{0,1},{1,0},{2,3},{3,2},{4,5},{5,4},{6,7},{7,6},{8,9},{9,8},{10,11... | collective-permute-start | bytes 786440 | tf_op jit(solution)/shard_map/ppermute | solution.py:305
  8.0 23.7 %collective-permute-start.1 = (bf16[2,512,128]{2,1,0:T(8,128)(2,1)S(1)}, bf16[2,512,128]{2,1,0:T(8,128)(2,1)S(1)}, u32[]{:S(2)}, u32[]{:S(2)}) collective-permute-start(bf16[2,512,128]{2,1,0:T(8,128)(2,1)S(1)} %get-tuple-element.97.own1), channel_id=1, source_target_pairs={{0,1},{1,0},{2,3},{3,2},{4,5},{5,4},{6,7},{7,6},{8,9},{9,8},{10,11... | collective-permute-start | bytes 786440 | tf_op jit(solution)/shard_map/ppermute | solution.py:305
  11.7 20.0 %collective-permute-start.5 = (bf16[2,512,128]{2,1,0:T(8,128)(2,1)S(1)}, bf16[2,512,128]{2,1,0:T(8,128)(2,1)S(1)}, u32[]{:S(2)}, u32[]{:S(2)}) collective-permute-start(bf16[2,512,128]{2,1,0:T(8,128)(2,1)S(1)} %get-tuple-element.98.own0), channel_id=1, source_target_pairs={{0,3},{3,0},{1,2},{2,1},{4,7},{7,4},{5,6},{6,5},{8,11},{11,8},{9,1... | collective-permute-start | bytes 786440 | tf_op jit(solution)/shard_map/ppermute | solution.py:305
  14.8 16.9 %collective-permute-start.4 = (bf16[2,512,128]{2,1,0:T(8,128)(2,1)S(1)}, bf16[2,512,128]{2,1,0:T(8,128)(2,1)S(1)}, u32[]{:S(2)}, u32[]{:S(2)}) collective-permute-start(bf16[2,512,128]{2,1,0:T(8,128)(2,1)S(1)} %collective-permute-done.3.back1), channel_id=1, source_target_pairs={{0,1},{1,0},{2,3},{3,2},{4,5},{5,4},{6,7},{7,6},{8,9},{9,8},{10,11... | collective-permute-start | bytes 786440 | tf_op jit(solution)/shard_map/ppermute | solution.py:305
  17.0 14.7 %collective-permute-start.2 = (bf16[2,512,128]{2,1,0:T(8,128)(2,1)S(1)}, bf16[2,512,128]{2,1,0:T(8,128)(2,1)S(1)}, u32[]{:S(2)}, u32[]{:S(2)}) collective-permute-start(bf16[2,512,128]{2,1,0:T(8,128)(2,1)S(1)} %collective-permute-done.side0), channel_id=1, source_target_pairs={{0,3},{3,0},{1,2},{2,1},{4,7},{7,4},{5,6},{6,5},{8,11},{11,8},{9,1... | collective-permute-start | bytes 786440 | tf_op jit(solution)/shard_map/ppermute | solution.py:305
  22.3 9.4 %all-to-all-start = ((f32[4,72,128]{2,1,0:T(8,128)}), f32[4,72,128]{2,1,0:T(8,128)S(1)}, u32[]{:S(2)}, u32[]{:S(2)}) async-start(f32[4,72,128]{2,1,0:T(8,128)} %pad_maximum_fusion), calls=%async_computation | async-start | bytes 294912 | tf_op jit(solution)/shard_map/all_to_all | solution.py:326
  43.1 10.0 %collective-permute-start.6 = (bf16[64,512]{1,0:T(8,128)(2,1)S(1)}, bf16[64,512]{1,0:T(8,128)(2,1)S(1)}, u32[]{:S(2)}, u32[]{:S(2)}) collective-permute-start(bf16[64,512]{1,0:T(8,128)(2,1)S(1)} %get-tuple-element.69), channel_id=1, source_target_pairs={{4,8},{8,4},{12,16},{16,12},{20,24},{24,20},{28,32},{32,28},{36,40... | collective-permute-start | bytes 196616 | tf_op jit(solution)/shard_map/ppermute | solution.py:356
  50.8 3.1 %collective-permute-start.7 = (bf16[64,512]{1,0:T(8,128)(2,1)S(1)}, bf16[64,512]{1,0:T(8,128)(2,1)S(1)}, u32[]{:S(2)}, u32[]{:S(2)}) collective-permute-start(bf16[64,512]{1,0:T(8,128)(2,1)S(1)} %get-tuple-element.70), channel_id=1, source_target_pairs={{0,4},{4,0},{8,12},{12,8},{16,20},{20,16},{24,28},{28,24},{32,36},... | collective-permute-start | bytes 196616 | tf_op jit(solution)/shard_map/ppermute | solution.py:357
  54.6 8.9 %collective-permute-start.8 = (bf16[64,512]{1,0:T(8,128)(2,1)S(1)}, bf16[64,512]{1,0:T(8,128)(2,1)S(1)}, u32[]{:S(2)}, u32[]{:S(2)}) collective-permute-start(bf16[64,512]{1,0:T(8,128)(2,1)S(1)} %get-tuple-element.76), channel_id=1, source_target_pairs={{4,8},{8,4},{12,16},{16,12},{20,24},{24,20},{28,32},{32,28},{36,40... | collective-permute-start | bytes 196616 | tf_op jit(solution)/shard_map/ppermute | solution.py:356
  60.4 3.1 %collective-permute-start.9 = (bf16[64,512]{1,0:T(8,128)(2,1)S(1)}, bf16[64,512]{1,0:T(8,128)(2,1)S(1)}, u32[]{:S(2)}, u32[]{:S(2)}) collective-permute-start(bf16[64,512]{1,0:T(8,128)(2,1)S(1)} %get-tuple-element.77), channel_id=1, source_target_pairs={{0,4},{4,0},{8,12},{12,8},{16,20},{20,16},{24,28},{28,24},{32,36},... | collective-permute-start | bytes 196616 | tf_op jit(solution)/shard_map/ppermute | solution.py:357
  64.3 8.9 %collective-permute-start.10 = (bf16[64,512]{1,0:T(8,128)(2,1)S(1)}, bf16[64,512]{1,0:T(8,128)(2,1)S(1)}, u32[]{:S(2)}, u32[]{:S(2)}) collective-permute-start(bf16[64,512]{1,0:T(8,128)(2,1)S(1)} %get-tuple-element.82), channel_id=1, source_target_pairs={{4,8},{8,4},{12,16},{16,12},{20,24},{24,20},{28,32},{32,28},{36,40... | collective-permute-start | bytes 196616 | tf_op jit(solution)/shard_map/ppermute | solution.py:356
  70.0 3.1 %collective-permute-start.11 = (bf16[64,512]{1,0:T(8,128)(2,1)S(1)}, bf16[64,512]{1,0:T(8,128)(2,1)S(1)}, u32[]{:S(2)}, u32[]{:S(2)}) collective-permute-start(bf16[64,512]{1,0:T(8,128)(2,1)S(1)} %get-tuple-element.83), channel_id=1, source_target_pairs={{0,4},{4,0},{8,12},{12,8},{16,20},{20,16},{24,28},{28,24},{32,36},... | collective-permute-start | bytes 196616 | tf_op jit(solution)/shard_map/ppermute | solution.py:357
  73.9 8.9 %collective-permute-start.12 = (bf16[64,512]{1,0:T(8,128)(2,1)S(1)}, bf16[64,512]{1,0:T(8,128)(2,1)S(1)}, u32[]{:S(2)}, u32[]{:S(2)}) collective-permute-start(bf16[64,512]{1,0:T(8,128)(2,1)S(1)} %get-tuple-element.88), channel_id=1, source_target_pairs={{4,8},{8,4},{12,16},{16,12},{20,24},{24,20},{28,32},{32,28},{36,40... | collective-permute-start | bytes 196616 | tf_op jit(solution)/shard_map/ppermute | solution.py:356
  79.6 3.1 %collective-permute-start.13 = (bf16[64,512]{1,0:T(8,128)(2,1)S(1)}, bf16[64,512]{1,0:T(8,128)(2,1)S(1)}, u32[]{:S(2)}, u32[]{:S(2)}) collective-permute-start(bf16[64,512]{1,0:T(8,128)(2,1)S(1)} %get-tuple-element.89), channel_id=1, source_target_pairs={{0,4},{4,0},{8,12},{12,8},{16,20},{20,16},{24,28},{28,24},{32,36},... | collective-permute-start | bytes 196616 | tf_op jit(solution)/shard_map/ppermute | solution.py:357
  83.5 8.9 %collective-permute-start.14 = (bf16[64,512]{1,0:T(8,128)(2,1)S(1)}, bf16[64,512]{1,0:T(8,128)(2,1)S(1)}, u32[]{:S(2)}, u32[]{:S(2)}) collective-permute-start(bf16[64,512]{1,0:T(8,128)(2,1)S(1)} %get-tuple-element.95), channel_id=1, source_target_pairs={{4,8},{8,4},{12,16},{16,12},{20,24},{24,20},{28,32},{32,28},{36,40... | collective-permute-start | bytes 196616 | tf_op jit(solution)/shard_map/ppermute | solution.py:356
  89.3 3.1 %collective-permute-start.15 = (bf16[64,512]{1,0:T(8,128)(2,1)S(1)}, bf16[64,512]{1,0:T(8,128)(2,1)S(1)}, u32[]{:S(2)}, u32[]{:S(2)}) collective-permute-start(bf16[64,512]{1,0:T(8,128)(2,1)S(1)} %get-tuple-element.96), channel_id=1, source_target_pairs={{0,4},{4,0},{8,12},{12,8},{16,20},{20,16},{24,28},{28,24},{32,36},... | collective-permute-start | bytes 196616 | tf_op jit(solution)/shard_map/ppermute | solution.py:357
